TPU v7x, 256 devices: a whole 4x4x8 slice. The times are simulated.
256 devices in a mesh: fsdp: 64 (over y, z, core), tensor: 4 (over x).
Axes of the slice: x: 4, y: 4, z: 8, core: 2. Of those that a mesh axis runs over, the one named last changes fastest.
Arguments:
- layer_input: bfloat16 [16384, 8192], P('fsdp', 'tensor'), may hold values from -6 to 6
- value_grad: bfloat16 [16384, 1024], P('fsdp', 'tensor'), may hold values from -6 to 6
- quant_codes: int32 [8192, 1024], P('fsdp', 'tensor'), may hold values from 0 to 15
- block_scales: float32 [8192, 16], P('fsdp', 'tensor'), may hold values from 0.02 to 0.08
- tenant_ids: int32 [1024], P('fsdp'), may hold values from 0 to 63
- live_counts: int32 [64], P('fsdp'), may hold values from 12 to 16, as said below
- tenant_owner: int32 [64], replicated, may hold values from 0 to 63, each once
- factor_down: float32 [64, 16, 8192], P('fsdp', None, 'tensor'), may hold values from -6 to 6
- factor_up: float32 [64, 16, 1024], P('fsdp', None, 'tensor'), may hold values from -6 to 6
- moment_down: float32 [64, 16, 8192], P('fsdp', None, 'tensor'), may hold values from -6 to 6
- second_down: float32 [64, 16, 8192], P('fsdp', None, 'tensor'), may hold values from 0.05 to 5
- moment_up: float32 [64, 16, 1024], P('fsdp', None, 'tensor'), may hold values from -6 to 6
- second_up: float32 [64, 16, 1024], P('fsdp', None, 'tensor'), may hold values from 0.05 to 5
Outputs:
- layer_input_gradient: bfloat16 [16384, 8192], P('fsdp', 'tensor')
- new_down: float32 [64, 16, 8192], P('fsdp', None, 'tensor')
- new_up: float32 [64, 16, 1024], P('fsdp', None, 'tensor')
- new_moment_down: float32 [64, 16, 8192], P('fsdp', None, 'tensor')
- new_second_down: float32 [64, 16, 8192], P('fsdp', None, 'tensor')
- new_moment_up: float32 [64, 16, 1024], P('fsdp', None, 'tensor')
- new_second_up: float32 [64, 16, 1024], P('fsdp', None, 'tensor')
Inputs may be any that keep to these rules, and one draw needn't show every extreme that they name: The first live_counts[f] sequence slots of fsdp index f are live and the rest are padding; some index has all 16 live. tenant_owner is a permutation: tenant t's adapter and its moments sit in slot tenant_owner[t].
All inputs are finite; a program needn't handle non-finite values.
Results may differ from a plain program's by a relative error of at most 0.01.
Values may be sent and summed in bfloat16 or wider, within the bound.
No kernel may reach another device: no remote copies, remote signals or barrier semaphores. Data moves between devices by JAX's collectives and lax.ppermute only.
A program may use at most 128 MiB of HBM per device.

v0:
```python
import math

import jax
import jax.numpy as jnp
from jax import lax
from jax.experimental import pallas as pl
from jax.experimental.pallas import tpu as pltpu
from jax.sharding import PartitionSpec as P

MODEL_WIDTH = 8192
ADAPTER_RANK = 16
NY, NZ, NC, NX = 4, 8, 2, 4


nf4_levels = (
    -1.0,
    -0.6962,
    -0.5251,
    -0.3949,
    -0.2844,
    -0.1848,
    -0.0911,
    0.0,
    0.0796,
    0.1609,
    0.2461,
    0.3379,
    0.4407,
    0.5626,
    0.723,
    1.0,
)
adapter_scale = 2.0
beta_one = 0.9
beta_two = 0.999
adam_step = 10.0
learn_rate = 0.05
decay_rate = 0.01
adam_eps = 1e-08
inverse_width = 1.0 / math.sqrt(MODEL_WIDTH)
coefficient = adapter_scale / math.sqrt(ADAPTER_RANK)


def flat_index(y, z, c, x):
    return ((y * NZ + z) * NC + c) * NX + x


def routed(value, route):
    pairs = []
    for y in range(NY):
        for z in range(NZ):
            for c in range(NC):
                for x in range(NX):
                    pairs.append((flat_index(y, z, c, x), flat_index(*route(y, z, c, x))))
    return lax.ppermute(value, ("fsdp", "tensor"), pairs)


def swap_cores(value):
    return routed(value, lambda y, z, c, x: (y, z, 1 - c, x))


def both_ways_z(value, k):
    return routed(value, lambda y, z, c, x: (y, (z + (k if c == 0 else -k)) % NZ, c, x))


def along_y(value, k):
    return routed(value, lambda y, z, c, x: ((y + k) % NY, z, c, x))


def along_x(value, k):
    return routed(value, lambda y, z, c, x: (y, z, c, (x + k) % NX))


def to_width_plane(value):
    return routed(value, lambda y, z, c, x: (x, z, c, y))


def adam_update(param, grad, moment, second):
    new_moment = beta_one * moment + (1.0 - beta_one) * grad
    new_second = beta_two * second + (1.0 - beta_two) * grad * grad
    corrected = new_moment / (1.0 - beta_one**adam_step)
    divisor = jnp.sqrt(new_second / (1.0 - beta_two**adam_step)) + adam_eps
    new_param = param - learn_rate * (corrected / divisor + decay_rate * param)
    return (new_param, new_moment, new_second)


def dequantize(quant_codes, block_scales):
    levels_out = jnp.zeros(quant_codes.shape, jnp.float32)
    for position in range(16):
        levels_out = jnp.where(quant_codes == position, nf4_levels[position], levels_out)
    row_count, col_count = quant_codes.shape
    blocks = block_scales.shape[1]
    scaled = levels_out.reshape(row_count, blocks, col_count // blocks) * block_scales[:, :, None]
    return scaled.reshape(row_count, col_count).astype(jnp.bfloat16)


def dot_nt(a, b):
    return lax.dot_general(a, b, (((1,), (1,)), ((), ())), preferred_element_type=jnp.float32)


def dot_nn(a, b):
    return lax.dot_general(a, b, (((1,), (0,)), ((), ())), preferred_element_type=jnp.float32)


PIECES = ((0, None), (1, 0), (1, 1), (2, 0), (2, 1), (3, 0), (3, 1), (4, None))


def chip_at(info, core, step):
    z = info[1]
    return jnp.where(core == 0, z - step, z + step) & 7


def block_of(info, core, piece):
    step, a = PIECES[piece]
    return chip_at(info, core, step) * 2 + (core if a is None else a)


def spread_rows(info, slots, low, jy):
    y, c = info[0], info[2]
    rows = []
    for piece in range(8):
        hit = slots == ((y - jy) & 3) * 16 + block_of(info, c, piece)
        rows.append(jnp.where(hit, low, jnp.zeros_like(low)))
    return jnp.concatenate(rows, axis=0)


def scores_body(info, slots_ref, x0, x1, d0, d1, a0, a1, a2, a3, out, acc):
    toks, width = x0.shape
    y, c = info[0], info[2]
    adapters = (a0, a1, a2, a3)
    for h, (xr, dr) in enumerate(((x0, d0), (x1, d1))):
        slots = slots_ref[:, h * toks : (h + 1) * toks]
        acc[1] = dot_nt(jnp.concatenate([a[:, width:] for a in adapters], axis=0), dr[...])
        acc[0] = jnp.zeros((512, toks), jnp.float32)

        @pl.loop(0, 2)
        def _(k, xr=xr):
            at = pl.ds(pl.multiple_of(k * 1024, 1024), 1024)
            acc[0] += dot_nt(jnp.concatenate([a[:, at] for a in adapters], axis=0), xr[:, at])

        in_sum = jnp.zeros((16, toks), jnp.float32)
        grad_sum = jnp.zeros((16, toks), jnp.float32)
        for jy in range(NY):
            for piece in range(8):
                hit = slots == ((y - jy) & 3) * 16 + block_of(info, c, piece)
                rows = slice(jy * 128 + piece * 16, jy * 128 + piece * 16 + 16)
                in_sum = in_sum + jnp.where(hit, acc[0, rows, :], 0.0)
                grad_sum = grad_sum + jnp.where(hit, acc[1, rows, :], 0.0)
        out[0:16, h * toks : (h + 1) * toks] = in_sum * inverse_width
        out[16:32, h * toks : (h + 1) * toks] = grad_sum * coefficient


def terms_body(info, slots_ref, low_ref, x0, x1, d0, d1, o0, o1, o2, o3, sg, si):
    toks, width = x0.shape
    outs = (o0, o1, o2, o3)
    for h in range(2):
        cols = slice(h * toks, (h + 1) * toks)
        slots = slots_ref[:, cols]
        low = low_ref[:, cols].astype(jnp.float32)
        for jy in range(NY):
            rows = slice(jy * 128, (jy + 1) * 128)
            sg[h, rows, :] = spread_rows(info, slots, low[16:32], jy).astype(jnp.bfloat16)
            si[h, rows, :] = spread_rows(info, slots, low[0:16], jy).astype(jnp.bfloat16)

    @pl.loop(0, width // 256)
    def _(k):
        at = pl.ds(pl.multiple_of(k * 256, 256), 256)
        down = dot_nn(sg[0], x0[:, at]) + dot_nn(sg[1], x1[:, at])
        down = (down * inverse_width).astype(jnp.bfloat16)
        for jy, out in enumerate(outs):
            out[:, at] = down[jy * 128 : (jy + 1) * 128]

    up = dot_nn(si[0], d0[...]) + dot_nn(si[1], d1[...])
    up = (up * coefficient).astype(jnp.bfloat16)
    for jy, out in enumerate(outs):
        out[:, width:] = up[jy * 128 : (jy + 1) * 128]


def y_sums_body(r0, r1, r2, r3, o0, o1, o2, o3, o4):
    at = 0
    for out in (o0, o1, o2, o3, o4):
        rows = slice(at, at + out.shape[0])
        total = r0[rows, :].astype(jnp.float32) + r1[rows, :].astype(jnp.float32)
        total = total + r2[rows, :].astype(jnp.float32) + r3[rows, :].astype(jnp.float32)
        out[...] = total.astype(out.dtype)
        at += out.shape[0]


def z_sums_body(info, p0, r1, r2, r3, r4, own, other):
    c = info[2]
    mine = pl.ds(pl.multiple_of(c * 16, 16), 16)
    theirs = pl.ds(pl.multiple_of((1 - c) * 16, 16), 16)
    total = p0[...] + r4[...].astype(jnp.float32)
    for r in (r1, r2, r3):
        total = total + r[mine, :].astype(jnp.float32)
    own[...] = total
    total = r1[theirs, :].astype(jnp.float32) + r2[theirs, :].astype(jnp.float32)
    other[...] = total + r3[theirs, :].astype(jnp.float32)


def back_body(info, slots_ref, low_ref, a0, a1, a2, a3, keep, send, spread, by_step):
    toks = slots_ref.shape[1] // 2
    c = info[2]
    for h in range(2):
        cols = slice(h * toks, (h + 1) * toks)
        slots = slots_ref[:, cols]
        low = low_ref[16:32, cols].astype(jnp.float32)
        for jy in range(NY):
            turned = spread_rows(info, slots, low, jy).T
            spread[cols, jy * 128 : (jy + 1) * 128] = turned.astype(jnp.bfloat16)

    @pl.loop(0, NZ)
    def _(step):
        at = pl.ds(pl.multiple_of(chip_at(info, c, step) * 256, 256), 256)
        part = jnp.concatenate([a[:, at] for a in (a0, a1, a2, a3)], axis=0)
        by_step[step] = (dot_nn(spread[...], part) * inverse_width).astype(jnp.bfloat16)

    for piece, (step, a) in enumerate(PIECES):
        to = slice(piece * 128, (piece + 1) * 128)
        if a is None:
            first, second = by_step[step, :, :128], by_step[step, :, 128:]
            keep[:, to] = jnp.where(c == 0, first, second)
            send[:, to] = jnp.where(c == 0, second, first)
        else:
            keep[:, to] = by_step[step, :, a * 128 : (a + 1) * 128]
            send[:, to] = by_step[8 - step, :, a * 128 : (a + 1) * 128]


def base_body(info, dv, *refs):
    y, x = info[0], info[3]
    *weights, out = refs
    out[...] = jnp.zeros_like(out)

    @pl.loop(0, NY)
    def _(q):
        grads = dv[(x - y + q) & 3]
        at = 0
        for w in weights:
            rows = w[q] if len(w.shape) == 3 else jnp.concatenate([w[0, q], w[1, q]], axis=0)
            out[:, at : at + rows.shape[0]] += dot_nt(grads, rows)
            at += rows.shape[0]


def finish_body(info, dv, w4, b01, b2, b3, keep, came, o0, o1, acc):
    toks = o0.shape[0]
    base_body(info, dv, w4, acc)
    for h, out in enumerate((o0, o1)):
        rows = slice(h * toks, (h + 1) * toks)
        turned = slice((1 - h) * toks, (2 - h) * toks)
        at = 0
        for base in (b01, b2, b3, acc):
            cols = slice(at, at + base.shape[1])
            total = base[rows, :] + keep[rows, cols].astype(jnp.float32)
            total = total + came[turned, cols].astype(jnp.float32)
            out[:, cols] = total.astype(jnp.bfloat16)
            at += base.shape[1]


def place_body(info, own, other, out):
    c = info[2]
    for core, ref in ((c, own), (1 - c, other)):
        for piece in range(8):
            at = pl.multiple_of(block_of(info, core, piece) * 128, 128)
            out[:, pl.ds(at, 128)] = ref[:, piece * 128 : (piece + 1) * 128]


SCALARS = pl.BlockSpec(memory_space=pltpu.SMEM)
LOCAL = pl.BlockSpec(memory_space=pltpu.VMEM)


def shape_of(shape, dtype):
    return jax.ShapeDtypeStruct(shape, dtype)


def call(body, operands, outs, flops, scalars=True, scratch=()):
    vmem_count = len(operands) - (1 if scalars else 0)
    moved = sum(o.size * o.dtype.itemsize for o in operands)
    moved += sum(math.prod(o.shape) * jnp.dtype(o.dtype).itemsize for o in outs)
    return pl.pallas_call(
        body,
        out_shape=outs,
        in_specs=([SCALARS] if scalars else []) + [LOCAL] * vmem_count,
        out_specs=[LOCAL] * len(outs),
        scratch_shapes=list(scratch),
        compiler_params=pltpu.CompilerParams(vmem_limit_bytes=24 * 1024 * 1024),
        cost_estimate=pl.CostEstimate(flops=flops, bytes_accessed=moved, transcendentals=0),
    )(*operands)


def shards(
    layer_input,
    value_grad,
    quant_codes,
    block_scales,
    tenant_ids,
    live_counts,
    tenant_owner,
    factor_down,
    factor_up,
    moment_down,
    second_down,
    moment_up,
    second_up,
):
    toks, width = layer_input.shape
    values = value_grad.shape[1]
    wide = width + values
    half = width // 2
    seqs = tenant_ids.shape[0]
    seq_len = toks // seqs
    place = lax.axis_index("fsdp") * NX + lax.axis_index("tensor")
    info = (place // jnp.array([64, 8, 4, 1], jnp.int32)) % jnp.array([4, 8, 2, 4], jnp.int32)
    first = (place // 4) % 2 == 0

    def in_order(own, other, axis=0):
        low = jnp.where(first, own, other)
        high = jnp.where(first, other, own)
        return jnp.concatenate([low, high], axis=axis)

    ab = jnp.concatenate([factor_down[0], factor_up[0]], axis=1).astype(jnp.bfloat16)
    chip_ab = in_order(ab, swap_cores(ab))
    steps = [both_ways_z(chip_ab, k) for k in range(1, 4)]
    az = jnp.concatenate([ab] + steps + [both_ways_z(ab, 4)], axis=0)
    adapters = [az] + [along_y(az, j) for j in range(1, NY)]

    matches = tenant_ids[:, None] == jnp.arange(tenant_owner.shape[0], dtype=jnp.int32)[None, :]
    slot_own = jnp.sum(jnp.where(matches, tenant_owner[None, :], 0), axis=1)
    slot_all = jnp.concatenate([slot_own, swap_cores(slot_own)])
    slots = jnp.broadcast_to(slot_all[:, None], (2 * seqs, seq_len)).reshape(1, 2 * toks)
    live_tok = jnp.arange(toks, dtype=jnp.int32) // seq_len < live_counts[0]
    d0 = jnp.where(live_tok[:, None], value_grad, jnp.zeros_like(value_grad))
    d1 = swap_cores(d0)
    x0, x1 = layer_input, swap_cores(layer_input)

    weight = to_width_plane(dequantize(quant_codes, block_scales))
    w0 = jnp.stack([weight] + [along_y(weight, j) for j in range(1, NY)])
    w1 = both_ways_z(in_order(w0[None], swap_cores(w0)[None]), 1)
    w2 = both_ways_z(w1, 1)
    w3 = both_ways_z(w2, 1)
    w4 = both_ways_z(jnp.where(first, w3[0], w3[1]), 1)
    chip_grad = jnp.concatenate([d0, d1], axis=0)
    dv = jnp.stack([chip_grad] + [along_x(chip_grad, j) for j in range(1, NX)])

    def base(*weights):
        columns = sum(w.size // 1024 for w in weights)
        return call(
            base_body,
            (info, dv, *weights),
            [shape_of((2 * toks, columns), jnp.float32)],
            2 * 2 * toks * columns * 1024,
        )[0]

    b01, b2, b3 = base(w0, w1), base(w2), base(w3)

    part = call(
        scores_body,
        (info, slots, x0, x1, d0, d1, *adapters),
        [shape_of((32, 2 * toks), jnp.float32)],
        2 * 2 * toks * 512 * wide,
        scratch=[pltpu.VMEM((2, 512, toks), jnp.float32)],
    )[0]
    pair = part[:, :toks] + swap_cores(part[:, toks:])
    low = pair
    for j in range(1, NX):
        low = low + along_x(pair, j)
    low = low.astype(jnp.bfloat16)
    low = jnp.concatenate([low, swap_cores(low)], axis=1)

    spread = pltpu.VMEM((2, 512, toks), jnp.bfloat16)
    terms = call(
        terms_body,
        (info, slots, low, x0, x1, d0, d1),
        [shape_of((128, wide), jnp.bfloat16)] * NY,
        2 * 2 * toks * 512 * wide,
        scratch=[spread, spread],
    )
    arrived = [terms[0]] + [along_y(terms[j], -j) for j in range(1, NY)]
    pieces = call(
        y_sums_body,
        tuple(arrived),
        [shape_of((16, wide), jnp.float32)]
        + [shape_of((32, wide), jnp.bfloat16)] * 3
        + [shape_of((16, wide), jnp.bfloat16)],
        4 * 128 * wide,
        scalars=False,
    )
    came = [both_ways_z(pieces[k], -k) for k in range(1, 5)]
    own, other = call(
        z_sums_body,
        (info, pieces[0], *came),
        [shape_of((16, wide), jnp.float32)] * 2,
        8 * 16 * wide,
    )
    gradient = own + swap_cores(other)
    down_gradient, up_gradient = gradient[None, :, :width], gradient[None, :, width:]
    new_down, new_moment_down, new_second_down = adam_update(
        factor_down, down_gradient, moment_down, second_down
    )
    new_up, new_moment_up, new_second_up = adam_update(factor_up, up_gradient, moment_up, second_up)

    keep, send = call(
        back_body,
        (info, slots, low, *adapters),
        [shape_of((2 * toks, half), jnp.bfloat16)] * 2,
        2 * 2 * toks * 512 * width,
        scratch=[
            pltpu.VMEM((2 * toks, 512), jnp.bfloat16),
            pltpu.VMEM((NZ, 2 * toks, 256), jnp.bfloat16),
        ],
    )
    o0, o1 = call(
        finish_body,
        (info, dv, w4, b01, b2, b3, keep, swap_cores(send)),
        [shape_of((toks, half), jnp.bfloat16)] * 2,
        2 * 2 * toks * 128 * 1024,
        scratch=[pltpu.VMEM((2 * toks, 128), jnp.float32)],
    )
    layer_input_gradient = call(
        place_body, (info, o0, swap_cores(o1)), [shape_of((toks, width), jnp.bfloat16)], 0
    )[0]
    return (
        layer_input_gradient,
        new_down,
        new_up,
        new_moment_down,
        new_second_down,
        new_moment_up,
        new_second_up,
    )


def solution(mesh):
    in_specs = (
        P("fsdp", "tensor"),
        P("fsdp", "tensor"),
        P("fsdp", "tensor"),
        P("fsdp", "tensor"),
        P("fsdp"),
        P("fsdp"),
        P(),
        P("fsdp", None, "tensor"),
        P("fsdp", None, "tensor"),
        P("fsdp", None, "tensor"),
        P("fsdp", None, "tensor"),
        P("fsdp", None, "tensor"),
        P("fsdp", None, "tensor"),
    )
    out_specs = (
        P("fsdp", "tensor"),
        P("fsdp", None, "tensor"),
        P("fsdp", None, "tensor"),
        P("fsdp", None, "tensor"),
        P("fsdp", None, "tensor"),
        P("fsdp", None, "tensor"),
        P("fsdp", None, "tensor"),
    )

    return jax.shard_map(shards, mesh=mesh, in_specs=in_specs, out_specs=out_specs, check_vma=False)
```

profile of v0, /device:TPU:1, one launch (start us, length us, event | category | flops | bytes accessed | tf_op | source)
XLA Modules:
  0.0 173.3 jit_solution(11903221697670398945)
XLA Ops:
  1.7 3.3 %collective-permute-start.15 = (bf16[16,2304]{1,0:T(8,128)(2,1)S(1)}, bf16[16,2304]{1,0:T(8,128)(2,1)S(1)}, u32[]{:S(2)}, u32[]{:S(2)}) collective-permute-start(bf16[16,2304]{1,0:T(8,128)(2,1)S(1)} %pad_maximum_fusion.5), channel_id=1, source_target_pairs={{0,4},{1,5},{2,6},{3,7},{4,0},{5,1},{6,2},{7,3},{8,12},{9,13},{10,... | collective-permute-start | bytes 221192 | tf_op jit(solution)/shard_map/ppermute | solution.py:55
  5.0 5.2 %collective-permute-start.19 = (bf16[16,2304]{1,0:T(8,128)(2,1)S(1)}, bf16[16,2304]{1,0:T(8,128)(2,1)S(1)}, u32[]{:S(2)}, u32[]{:S(2)}) collective-permute-start(bf16[16,2304]{1,0:T(8,128)(2,1)S(1)} %pad_maximum_fusion.5), channel_id=1, source_target_pairs={{0,32},{1,33},{2,34},{3,35},{4,36},{5,37},{6,38},{7,39},{8,40},{9,... | collective-permute-start | bytes 221192 | tf_op jit(solution)/shard_map/ppermute | solution.py:55
  14.4 4.8 %collective-permute-start.5 = (bf16[128,256]{1,0:T(8,128)(2,1)S(1)}, bf16[128,256]{1,0:T(8,128)(2,1)S(1)}, u32[]{:S(2)}, u32[]{:S(2)}) collective-permute-start(bf16[128,256]{1,0:T(8,128)(2,1)S(1)} %collective-permute-done.4), channel_id=1, source_target_pairs={{0,64},{1,65},{2,66},{3,67},{4,68},{5,69},{6,70},{7,71},{8,72},{9,... | collective-permute-start | bytes 196616 | tf_op jit(solution)/shard_map/ppermute | solution.py:55
  19.2 6.9 %collective-permute-start.6 = (bf16[128,256]{1,0:T(8,128)(2,1)S(1)}, bf16[128,256]{1,0:T(8,128)(2,1)S(1)}, u32[]{:S(2)}, u32[]{:S(2)}) collective-permute-start(bf16[128,256]{1,0:T(8,128)(2,1)S(1)} %collective-permute-done.4), channel_id=1, source_target_pairs={{0,128},{1,129},{2,130},{3,131},{4,132},{5,133},{6,134},{7,135},{8... | collective-permute-start | bytes 196616 | tf_op jit(solution)/shard_map/ppermute | solution.py:55
  27.0 2.8 %collective-permute-start = (bf16[256,256]{1,0:T(8,128)(2,1)S(1)}, bf16[256,256]{1,0:T(8,128)(2,1)S(1)}, u32[]{:S(2)}, u32[]{:S(2)}) collective-permute-start(bf16[256,256]{1,0:T(8,128)(2,1)S(1)} %broadcast_select_fusion.d0), channel_id=1, source_target_pairs={{0,4},{1,5},{2,6},{3,7},{4,0},{5,1},{6,2},{7,3},{8,12},{9,13},{10,... | collective-permute-start | bytes 393224 | tf_op jit(solution)/shard_map/ppermute | solution.py:55
  30.6 1.3 collective-permute-start.14
  32.1 6.4 %collective-permute-done.17 = bf16[32,2304]{1,0:T(8,128)(2,1)S(1)} collective-permute-done((bf16[32,2304]{1,0:T(8,128)(2,1)S(1)}, bf16[32,2304]{1,0:T(8,128)(2,1)S(1)}, u32[]{:S(2)}, u32[]{:S(2)}) %collective-permute-start.17) | collective-permute-done | bytes 147488 | tf_op jit(solution)/shard_map/ppermute | solution.py:55
  38.9 7.2 %collective-permute-done.18 = bf16[32,2304]{1,0:T(8,128)(2,1)S(1)} collective-permute-done((bf16[32,2304]{1,0:T(8,128)(2,1)S(1)}, bf16[32,2304]{1,0:T(8,128)(2,1)S(1)}, u32[]{:S(2)}, u32[]{:S(2)}) %collective-permute-start.18) | collective-permute-done | bytes 147488 | tf_op jit(solution)/shard_map/ppermute | solution.py:55
  46.1 6.4 %collective-permute-start.8 = (bf16[4,128,256]{2,1,0:T(8,128)(2,1)S(1)}, bf16[4,128,256]{2,1,0:T(8,128)(2,1)S(1)}, u32[]{:S(2)}, u32[]{:S(2)}) collective-permute-start(bf16[4,128,256]{2,1,0:T(8,128)(2,1)S(1)} %pad_maximum_fusion.3.refs_0_), channel_id=1, source_target_pairs={{0,4},{1,5},{2,6},{3,7},{4,0},{5,1},{6,2},{7,3},{8,12},{9,13},{10,... | collective-permute-start | bytes 786440 | tf_op jit(solution)/shard_map/ppermute | solution.py:55
  53.6 2.5 %collective-permute-start.22 = (bf16[128,2304]{1,0:T(8,128)(2,1)S(1)}, bf16[128,2304]{1,0:T(8,128)(2,1)}, u32[]{:S(2)}, u32[]{:S(2)}) collective-permute-start(bf16[128,2304]{1,0:T(8,128)(2,1)S(1)} %constant_dynamic-update-slice_fusion.a0), channel_id=1, source_target_pairs={{0,192},{1,193},{2,194},{3,195},{4,196},{5,197},{6,198},{7,199},{8... | collective-permute-start | bytes 1769480 | tf_op jit(solution)/shard_map/ppermute | solution.py:55
  57.5 23.8 %collective-permute-done.20.a1 = bf16[128,2304]{1,0:T(8,128)(2,1)} collective-permute-done((bf16[128,2304]{1,0:T(8,128)(2,1)S(1)}, bf16[128,2304]{1,0:T(8,128)(2,1)}, u32[]{:S(2)}, u32[]{:S(2)}) %collective-permute-start.20) | collective-permute-done | bytes 589856 | tf_op jit(solution)/shard_map/ppermute | solution.py:55
  81.7 4.0 %shard_map.201 = f32[32,512]{1,0:T(8,128)S(1)} custom-call(s32[4]{0:T(128)S(1)} %and_select_fusion.1.info, s32[1,512]{1,0:T(1,128)S(1)} %reshape.48.slots_ref, bf16[256,2048]{1,0:T(8,128)(2,1)S(1)} %copy-done, bf16[256,2048]{1,0:T(8,128)(2,1)S(1)} %collective-permute-done.14.x1, bf16[256,256]{1,0:T(8,128)(2,1)S(1)} %broadcast_select_fusion.d0, ...), custom_call_target="tpu_custom_call" | custom-call | flops 1207959552 | bytes 4786192 | tf_op jit(solution)/shard_map/pallas_call | solution.py:279
  87.8 2.1 %collective-permute-start.25 = (f32[32,256]{1,0:T(8,128)S(1)}, f32[32,256]{1,0:T(8,128)S(1)}, u32[]{:S(2)}, u32[]{:S(2)}) collective-permute-start(f32[32,256]{1,0:T(8,128)S(1)} %slice_add_fusion), channel_id=1, source_target_pairs={{0,2},{1,3},{2,0},{3,1},{4,6},{5,7},{6,4},{7,5},{8,10},{9,11},{10,... | collective-permute-start | bytes 98312 | tf_op jit(solution)/shard_map/ppermute | solution.py:55
  93.0 1.8 %collective-permute-start.27 = (bf16[32,256]{1,0:T(8,128)(2,1)S(1)}, bf16[32,256]{1,0:T(8,128)(2,1)S(1)}, u32[]{:S(2)}, u32[]{:S(2)}) collective-permute-start(bf16[32,256]{1,0:T(8,128)(2,1)S(1)} %add_convert_fusion), channel_id=1, source_target_pairs={{0,4},{1,5},{2,6},{3,7},{4,0},{5,1},{6,2},{7,3},{8,12},{9,13},{10,... | collective-permute-start | bytes 49160 | tf_op jit(solution)/shard_map/ppermute | solution.py:55
  95.6 3.5 %shard_map.205 = (bf16[128,2304]{1,0:T(8,128)(2,1)S(1)}, bf16[128,2304]{1,0:T(8,128)(2,1)S(1)}, bf16[128,2304]{1,0:T(8,128)(2,1)S(1)}, bf16[128,2304]{1,0:T(8,128)(2,1)S(1)}) custom-call(s32[4]{0:T(128)S(1)} %and_select_fusion.1.info, s32[1,512]{1,0:T(1,128)S(1)} %reshape.48.slots_ref, bf16[32,512]{1,0:T(8,128)(2,1)S(1)} %pad_maximum_fusion.6.low_ref, ...), custom_call_target="tpu_custom_call" | custom-call | flops 1207959552 | bytes 4753424 | tf_op jit(solution)/shard_map/pallas_call | solution.py:279
  99.1 2.4 %collective-permute-start.30 = (bf16[128,2304]{1,0:T(8,128)(2,1)S(1)}, bf16[128,2304]{1,0:T(8,128)(2,1)S(1)}, u32[]{:S(2)}, u32[]{:S(2)}) collective-permute-start(bf16[128,2304]{1,0:T(8,128)(2,1)S(1)} %get-tuple-element.27), channel_id=1, source_target_pairs={{0,192},{1,193},{2,194},{3,195},{4,196},{5,197},{6,198},{7,199},{8... | collective-permute-start | bytes 1769480 | tf_op jit(solution)/shard_map/ppermute | solution.py:55
  102.5 4.4 %shard_map.202 = (bf16[512,1024]{1,0:T(8,128)(2,1)S(1)}, bf16[512,1024]{1,0:T(8,128)(2,1)S(1)}) custom-call(s32[4]{0:T(128)S(1)} %and_select_fusion.1.info, s32[1,512]{1,0:T(1,128)S(1)} %reshape.48.slots_ref, bf16[32,512]{1,0:T(8,128)(2,1)S(1)} %pad_maximum_fusion.6.low_ref, bf16[128,2304]{1,0:T(8,128)(2,1)S(1)} %constant_dynamic-update-slice_fusion.a0, ...), custom_call_target="tpu_custom_call" | custom-call | flops 1073741824 | bytes 4491280 | tf_op jit(solution)/shard_map/pallas_call | solution.py:279
  108.6 5.9 %collective-permute-done.30.r1 = bf16[128,2304]{1,0:T(8,128)(2,1)S(1)} collective-permute-done((bf16[128,2304]{1,0:T(8,128)(2,1)S(1)}, bf16[128,2304]{1,0:T(8,128)(2,1)S(1)}, u32[]{:S(2)}, u32[]{:S(2)}) %collective-permute-start.30) | collective-permute-done | bytes 589856 | tf_op jit(solution)/shard_map/ppermute | solution.py:55
  114.6 2.8 %collective-permute-done.31.r2 = bf16[128,2304]{1,0:T(8,128)(2,1)S(1)} collective-permute-done((bf16[128,2304]{1,0:T(8,128)(2,1)S(1)}, bf16[128,2304]{1,0:T(8,128)(2,1)S(1)}, u32[]{:S(2)}, u32[]{:S(2)}) %collective-permute-start.31) | collective-permute-done | bytes 589856 | tf_op jit(solution)/shard_map/ppermute | solution.py:55
  117.4 13.6 %collective-permute-done.32.r3 = bf16[128,2304]{1,0:T(8,128)(2,1)S(1)} collective-permute-done((bf16[128,2304]{1,0:T(8,128)(2,1)S(1)}, bf16[128,2304]{1,0:T(8,128)(2,1)S(1)}, u32[]{:S(2)}, u32[]{:S(2)}) %collective-permute-start.32) | collective-permute-done | bytes 589856 | tf_op jit(solution)/shard_map/ppermute | solution.py:55
  132.2 2.6 %collective-permute-start.36 = (bf16[16,2304]{1,0:T(8,128)(2,1)S(1)}, bf16[16,2304]{1,0:T(8,128)(2,1)S(1)}, u32[]{:S(2)}, u32[]{:S(2)}) collective-permute-start(bf16[16,2304]{1,0:T(8,128)(2,1)S(1)} %get-tuple-element.34), channel_id=1, source_target_pairs={{0,32},{1,33},{2,34},{3,35},{4,36},{5,37},{6,38},{7,39},{8,40},{9,... | collective-permute-start | bytes 221192 | tf_op jit(solution)/shard_map/ppermute | solution.py:55
  134.8 6.6 %collective-permute-done.36.r4 = bf16[16,2304]{1,0:T(8,128)(2,1)S(1)} collective-permute-done((bf16[16,2304]{1,0:T(8,128)(2,1)S(1)}, bf16[16,2304]{1,0:T(8,128)(2,1)S(1)}, u32[]{:S(2)}, u32[]{:S(2)}) %collective-permute-start.36) | collective-permute-done | bytes 73760 | tf_op jit(solution)/shard_map/ppermute | solution.py:55
  142.6 2.1 %collective-permute-start.2 = (bf16[512,256]{1,0:T(8,128)(2,1)S(1)}, bf16[512,256]{1,0:T(8,128)(2,1)S(1)}, u32[]{:S(2)}, u32[]{:S(2)}) collective-permute-start(bf16[512,256]{1,0:T(8,128)(2,1)S(1)} %get-tuple-element.46), channel_id=1, source_target_pairs={{0,2},{1,3},{2,0},{3,1},{4,6},{5,7},{6,4},{7,5},{8,10},{9,11},{10,... | collective-permute-start | bytes 786440 | tf_op jit(solution)/shard_map/ppermute | solution.py:55
  145.0 1.3 collective-permute-start.35
  146.3 6.9 %collective-permute-done.35.r3 = bf16[32,2304]{1,0:T(8,128)(2,1)S(1)} collective-permute-done((bf16[32,2304]{1,0:T(8,128)(2,1)S(1)}, bf16[32,2304]{1,0:T(8,128)(2,1)S(1)}, u32[]{:S(2)}, u32[]{:S(2)}) %collective-permute-start.35) | collective-permute-done | bytes 147488 | tf_op jit(solution)/shard_map/ppermute | solution.py:55
  153.2 2.5 %collective-permute-start.12 = (bf16[4,128,256]{2,1,0:T(8,128)(2,1)S(1)}, bf16[4,128,256]{2,1,0:T(8,128)(2,1)S(1)}, u32[]{:S(2)}, u32[]{:S(2)}) collective-permute-start(bf16[4,128,256]{2,1,0:T(8,128)(2,1)S(1)} %fusion), channel_id=1, source_target_pairs={{0,8},{1,9},{2,10},{3,11},{4,60},{5,61},{6,62},{7,63},{8,16},{9,17... | collective-permute-start | bytes 786440 | tf_op jit(solution)/shard_map/ppermute | solution.py:55
  156.4 5.4 %collective-permute-start.37 = (f32[16,2304]{1,0:T(8,128)S(1)}, f32[16,2304]{1,0:T(8,128)S(1)}, u32[]{:S(2)}, u32[]{:S(2)}) collective-permute-start(f32[16,2304]{1,0:T(8,128)S(1)} %get-tuple-element.36), channel_id=1, source_target_pairs={{0,4},{1,5},{2,6},{3,7},{4,0},{5,1},{6,2},{7,3},{8,12},{9,13},{10,... | collective-permute-start | bytes 442376 | tf_op jit(solution)/shard_map/ppermute | solution.py:55
  161.9 2.3 %shard_map.198.b01 = f32[512,384]{1,0:T(8,128)S(1)} custom-call(s32[4]{0:T(128)S(1)} %and_select_fusion.1.info, bf16[4,512,256]{2,1,0:T(8,128)(2,1)S(1)} %pad_maximum_fusion.dv, bf16[4,128,256]{2,1,0:T(8,128)(2,1)S(1)} %pad_maximum_fusion.3.refs_0_, bf16[2,4,128,256]{3,2,1,0:T(8,128)(2,1)} %collective-permute-done.9.refs_1_), custom_call_target="tpu_custom_call" | custom-call | flops 402653184 | bytes 2621456 | tf_op jit(solution)/shard_map/pallas_call | solution.py:279
  164.3 1.6 shard_map.199.b2
  165.9 1.6 shard_map.200.b3
  167.7 1.8 %shard_map.203 = (bf16[256,1024]{1,0:T(8,128)(2,1)S(1)}, bf16[256,1024]{1,0:T(8,128)(2,1)S(1)}) custom-call(s32[4]{0:T(128)S(1)} %and_select_fusion.1.info, bf16[4,512,256]{2,1,0:T(8,128)(2,1)S(1)} %pad_maximum_fusion.dv, bf16[4,128,256]{2,1,0:T(8,128)(2,1)S(1)} %collective-permute-done.12.w4, f32[512,384]{1,0:T(8,128)S(1)} %shard_map.198.b01, ...), custom_call_target="tpu_custom_call" | custom-call | flops 134217728 | bytes 6291472 | tf_op jit(solution)/shard_map/pallas_call | solution.py:279
  171.5 1.8 %shard_map.204 = bf16[256,2048]{1,0:T(8,128)(2,1)} custom-call(s32[4]{0:T(128)S(1)} %and_select_fusion.1.info, bf16[256,1024]{1,0:T(8,128)(2,1)S(1)} %get-tuple-element.24.own, bf16[256,1024]{1,0:T(8,128)(2,1)S(1)} %collective-permute-done.29.other), custom_call_target="tpu_custom_call" | custom-call | bytes 2097168 | tf_op jit(solution)/shard_map/pallas_call | solution.py:279
  (108 shorter events, 23.9 us)
Async XLA Ops:
  1.7 24.4 %collective-permute-start.15 = (bf16[16,2304]{1,0:T(8,128)(2,1)S(1)}, bf16[16,2304]{1,0:T(8,128)(2,1)S(1)}, u32[]{:S(2)}, u32[]{:S(2)}) collective-permute-start(bf16[16,2304]{1,0:T(8,128)(2,1)S(1)} %pad_maximum_fusion.5), channel_id=1, source_target_pairs={{0,4},{1,5},{2,6},{3,7},{4,0},{5,1},{6,2},{7,3},{8,12},{9,13},{10,... | collective-permute-start | bytes 221192 | tf_op jit(solution)/shard_map/ppermute | solution.py:55
  5.0 47.4 %collective-permute-start.19 = (bf16[16,2304]{1,0:T(8,128)(2,1)S(1)}, bf16[16,2304]{1,0:T(8,128)(2,1)S(1)}, u32[]{:S(2)}, u32[]{:S(2)}) collective-permute-start(bf16[16,2304]{1,0:T(8,128)(2,1)S(1)} %pad_maximum_fusion.5), channel_id=1, source_target_pairs={{0,32},{1,33},{2,34},{3,35},{4,36},{5,37},{6,38},{7,39},{8,40},{9,... | collective-permute-start | bytes 221192 | tf_op jit(solution)/shard_map/ppermute | solution.py:55
  14.4 12.6 %collective-permute-start.5 = (bf16[128,256]{1,0:T(8,128)(2,1)S(1)}, bf16[128,256]{1,0:T(8,128)(2,1)S(1)}, u32[]{:S(2)}, u32[]{:S(2)}) collective-permute-start(bf16[128,256]{1,0:T(8,128)(2,1)S(1)} %collective-permute-done.4), channel_id=1, source_target_pairs={{0,64},{1,65},{2,66},{3,67},{4,68},{5,69},{6,70},{7,71},{8,72},{9,... | collective-permute-start | bytes 196616 | tf_op jit(solution)/shard_map/ppermute | solution.py:55
  19.2 10.5 %collective-permute-start.6 = (bf16[128,256]{1,0:T(8,128)(2,1)S(1)}, bf16[128,256]{1,0:T(8,128)(2,1)S(1)}, u32[]{:S(2)}, u32[]{:S(2)}) collective-permute-start(bf16[128,256]{1,0:T(8,128)(2,1)S(1)} %collective-permute-done.4), channel_id=1, source_target_pairs={{0,128},{1,129},{2,130},{3,131},{4,132},{5,133},{6,134},{7,135},{8... | collective-permute-start | bytes 196616 | tf_op jit(solution)/shard_map/ppermute | solution.py:55
  26.1 4.5 %collective-permute-start.7 = (bf16[128,256]{1,0:T(8,128)(2,1)S(1)}, bf16[128,256]{1,0:T(8,128)(2,1)S(1)}, u32[]{:S(2)}, u32[]{:S(2)}) collective-permute-start(bf16[128,256]{1,0:T(8,128)(2,1)S(1)} %collective-permute-done.4), channel_id=1, source_target_pairs={{0,192},{1,193},{2,194},{3,195},{4,196},{5,197},{6,198},{7,199},{8... | collective-permute-start | bytes 196616 | tf_op jit(solution)/shard_map/ppermute | solution.py:55
  26.2 5.8 %collective-permute-start.16 = (bf16[32,2304]{1,0:T(8,128)(2,1)S(1)}, bf16[32,2304]{1,0:T(8,128)(2,1)S(1)}, u32[]{:S(2)}, u32[]{:S(2)}) collective-permute-start(bf16[32,2304]{1,0:T(8,128)(2,1)S(1)} %pad_maximum_fusion.4), channel_id=1, source_target_pairs={{0,8},{1,9},{2,10},{3,11},{4,60},{5,61},{6,62},{7,63},{8,16},{9,17... | collective-permute-start | bytes 442376 | tf_op jit(solution)/shard_map/ppermute | solution.py:55
  27.0 30.0 %collective-permute-start = (bf16[256,256]{1,0:T(8,128)(2,1)S(1)}, bf16[256,256]{1,0:T(8,128)(2,1)S(1)}, u32[]{:S(2)}, u32[]{:S(2)}) collective-permute-start(bf16[256,256]{1,0:T(8,128)(2,1)S(1)} %broadcast_select_fusion.d0), channel_id=1, source_target_pairs={{0,4},{1,5},{2,6},{3,7},{4,0},{5,1},{6,2},{7,3},{8,12},{9,13},{10,... | collective-permute-start | bytes 393224 | tf_op jit(solution)/shard_map/ppermute | solution.py:55
  29.8 23.8 %collective-permute-start.13 = (s32[16]{0:T(128)S(1)}, s32[16]{0:T(128)S(1)}, u32[]{:S(2)}, u32[]{:S(2)}) collective-permute-start(s32[16]{0:T(128)S(1)} %select_reduce_fusion), channel_id=1, source_target_pairs={{0,4},{1,5},{2,6},{3,7},{4,0},{5,1},{6,2},{7,3},{8,12},{9,13},{10,... | collective-permute-start | bytes 200 | tf_op jit(solution)/shard_map/ppermute | solution.py:55
  30.6 51.1 %collective-permute-start.14 = (bf16[256,2048]{1,0:T(8,128)(2,1)S(1)}, bf16[256,2048]{1,0:T(8,128)(2,1)S(1)}, u32[]{:S(2)}, u32[]{:S(2)}) collective-permute-start(bf16[256,2048]{1,0:T(8,128)(2,1)S(1)} %copy-done), channel_id=1, source_target_pairs={{0,4},{1,5},{2,6},{3,7},{4,0},{5,1},{6,2},{7,3},{8,12},{9,13},{10,... | collective-permute-start | bytes 3145736 | tf_op jit(solution)/shard_map/ppermute | solution.py:55
  32.0 6.6 %collective-permute-start.17 = (bf16[32,2304]{1,0:T(8,128)(2,1)S(1)}, bf16[32,2304]{1,0:T(8,128)(2,1)S(1)}, u32[]{:S(2)}, u32[]{:S(2)}) collective-permute-start(bf16[32,2304]{1,0:T(8,128)(2,1)S(1)} %pad_maximum_fusion.4), channel_id=1, source_target_pairs={{0,16},{1,17},{2,18},{3,19},{4,52},{5,53},{6,54},{7,55},{8,24},{9,... | collective-permute-start | bytes 442376 | tf_op jit(solution)/shard_map/ppermute | solution.py:55
  38.5 7.6 %collective-permute-start.18 = (bf16[32,2304]{1,0:T(8,128)(2,1)S(1)}, bf16[32,2304]{1,0:T(8,128)(2,1)S(1)}, u32[]{:S(2)}, u32[]{:S(2)}) collective-permute-start(bf16[32,2304]{1,0:T(8,128)(2,1)S(1)} %pad_maximum_fusion.4), channel_id=1, source_target_pairs={{0,24},{1,25},{2,26},{3,27},{4,44},{5,45},{6,46},{7,47},{8,32},{9,... | collective-permute-start | bytes 442376 | tf_op jit(solution)/shard_map/ppermute | solution.py:55
  46.1 7.5 %collective-permute-start.8 = (bf16[4,128,256]{2,1,0:T(8,128)(2,1)S(1)}, bf16[4,128,256]{2,1,0:T(8,128)(2,1)S(1)}, u32[]{:S(2)}, u32[]{:S(2)}) collective-permute-start(bf16[4,128,256]{2,1,0:T(8,128)(2,1)S(1)} %pad_maximum_fusion.3.refs_0_), channel_id=1, source_target_pairs={{0,4},{1,5},{2,6},{3,7},{4,0},{5,1},{6,2},{7,3},{8,12},{9,13},{10,... | collective-permute-start | bytes 786440 | tf_op jit(solution)/shard_map/ppermute | solution.py:55
  52.4 28.9 %collective-permute-start.20 = (bf16[128,2304]{1,0:T(8,128)(2,1)S(1)}, bf16[128,2304]{1,0:T(8,128)(2,1)}, u32[]{:S(2)}, u32[]{:S(2)}) collective-permute-start(bf16[128,2304]{1,0:T(8,128)(2,1)S(1)} %constant_dynamic-update-slice_fusion.a0), channel_id=1, source_target_pairs={{0,64},{1,65},{2,66},{3,67},{4,68},{5,69},{6,70},{7,71},{8,72},{9,... | collective-permute-start | bytes 1769480 | tf_op jit(solution)/shard_map/ppermute | solution.py:55
  53.6 27.8 %collective-permute-start.21 = (bf16[128,2304]{1,0:T(8,128)(2,1)S(1)}, bf16[128,2304]{1,0:T(8,128)(2,1)}, u32[]{:S(2)}, u32[]{:S(2)}) collective-permute-start(bf16[128,2304]{1,0:T(8,128)(2,1)S(1)} %constant_dynamic-update-slice_fusion.a0), channel_id=1, source_target_pairs={{0,128},{1,129},{2,130},{3,131},{4,132},{5,133},{6,134},{7,135},{8... | collective-permute-start | bytes 1769480 | tf_op jit(solution)/shard_map/ppermute | solution.py:55
  53.6 28.1 %collective-permute-start.22 = (bf16[128,2304]{1,0:T(8,128)(2,1)S(1)}, bf16[128,2304]{1,0:T(8,128)(2,1)}, u32[]{:S(2)}, u32[]{:S(2)}) collective-permute-start(bf16[128,2304]{1,0:T(8,128)(2,1)S(1)} %constant_dynamic-update-slice_fusion.a0), channel_id=1, source_target_pairs={{0,192},{1,193},{2,194},{3,195},{4,196},{5,197},{6,198},{7,199},{8... | collective-permute-start | bytes 1769480 | tf_op jit(solution)/shard_map/ppermute | solution.py:55
  57.0 33.7 %collective-permute-start.9 = (bf16[2,4,128,256]{3,2,1,0:T(8,128)(2,1)}, bf16[2,4,128,256]{3,2,1,0:T(8,128)(2,1)}, u32[]{:S(2)}, u32[]{:S(2)}) collective-permute-start(bf16[2,4,128,256]{3,2,1,0:T(8,128)(2,1)} %pad_maximum_fusion.1), channel_id=1, source_target_pairs={{0,8},{1,9},{2,10},{3,11},{4,60},{5,61},{6,62},{7,63},{8,16},{9,17... | collective-permute-start | bytes 1572872 | tf_op jit(solution)/shard_map/ppermute | solution.py:55
  87.8 4.6 %collective-permute-start.25 = (f32[32,256]{1,0:T(8,128)S(1)}, f32[32,256]{1,0:T(8,128)S(1)}, u32[]{:S(2)}, u32[]{:S(2)}) collective-permute-start(f32[32,256]{1,0:T(8,128)S(1)} %slice_add_fusion), channel_id=1, source_target_pairs={{0,2},{1,3},{2,0},{3,1},{4,6},{5,7},{6,4},{7,5},{8,10},{9,11},{10,... | collective-permute-start | bytes 98312 | tf_op jit(solution)/shard_map/ppermute | solution.py:55
  90.7 17.5 %collective-permute-start.10 = (bf16[2,4,128,256]{3,2,1,0:T(8,128)(2,1)}, bf16[2,4,128,256]{3,2,1,0:T(8,128)(2,1)S(1)}, u32[]{:S(2)}, u32[]{:S(2)}) collective-permute-start(bf16[2,4,128,256]{3,2,1,0:T(8,128)(2,1)} %collective-permute-done.9.refs_1_), channel_id=1, source_target_pairs={{0,8},{1,9},{2,10},{3,11},{4,60},{5,61},{6,62},{7,63},{8,16},{9,17... | collective-permute-start | bytes 1572872 | tf_op jit(solution)/shard_map/ppermute | solution.py:55
  99.1 15.4 %collective-permute-start.30 = (bf16[128,2304]{1,0:T(8,128)(2,1)S(1)}, bf16[128,2304]{1,0:T(8,128)(2,1)S(1)}, u32[]{:S(2)}, u32[]{:S(2)}) collective-permute-start(bf16[128,2304]{1,0:T(8,128)(2,1)S(1)} %get-tuple-element.27), channel_id=1, source_target_pairs={{0,192},{1,193},{2,194},{3,195},{4,196},{5,197},{6,198},{7,199},{8... | collective-permute-start | bytes 1769480 | tf_op jit(solution)/shard_map/ppermute | solution.py:55
  101.6 15.8 %collective-permute-start.31 = (bf16[128,2304]{1,0:T(8,128)(2,1)S(1)}, bf16[128,2304]{1,0:T(8,128)(2,1)S(1)}, u32[]{:S(2)}, u32[]{:S(2)}) collective-permute-start(bf16[128,2304]{1,0:T(8,128)(2,1)S(1)} %get-tuple-element.28), channel_id=1, source_target_pairs={{0,128},{1,129},{2,130},{3,131},{4,132},{5,133},{6,134},{7,135},{8... | collective-permute-start | bytes 1769480 | tf_op jit(solution)/shard_map/ppermute | solution.py:55
  102.4 28.5 %collective-permute-start.32 = (bf16[128,2304]{1,0:T(8,128)(2,1)S(1)}, bf16[128,2304]{1,0:T(8,128)(2,1)S(1)}, u32[]{:S(2)}, u32[]{:S(2)}) collective-permute-start(bf16[128,2304]{1,0:T(8,128)(2,1)S(1)} %get-tuple-element.29), channel_id=1, source_target_pairs={{0,64},{1,65},{2,66},{3,67},{4,68},{5,69},{6,70},{7,71},{8,72},{9,... | collective-permute-start | bytes 1769480 | tf_op jit(solution)/shard_map/ppermute | solution.py:55
  106.9 60.6 %collective-permute-start.28 = (bf16[512,1024]{1,0:T(8,128)(2,1)S(1)}, bf16[512,1024]{1,0:T(8,128)(2,1)S(1)}, u32[]{:S(2)}, u32[]{:S(2)}) collective-permute-start(bf16[512,1024]{1,0:T(8,128)(2,1)S(1)} %get-tuple-element.23), channel_id=1, source_target_pairs={{0,4},{1,5},{2,6},{3,7},{4,0},{5,1},{6,2},{7,3},{8,12},{9,13},{10,... | collective-permute-start | bytes 3145736 | tf_op jit(solution)/shard_map/ppermute | solution.py:55
  108.2 36.8 %collective-permute-start.11 = (bf16[2,4,128,256]{3,2,1,0:T(8,128)(2,1)S(1)}, bf16[2,4,128,256]{3,2,1,0:T(8,128)(2,1)S(1)}, u32[]{:S(2)}, u32[]{:S(2)}) collective-permute-start(bf16[2,4,128,256]{3,2,1,0:T(8,128)(2,1)S(1)} %collective-permute-done.10.refs_0_), channel_id=1, source_target_pairs={{0,8},{1,9},{2,10},{3,11},{4,60},{5,61},{6,62},{7,63},{8,16},{9,17... | collective-permute-start | bytes 1572872 | tf_op jit(solution)/shard_map/ppermute | solution.py:55
  131.2 11.3 %collective-permute-start.33 = (bf16[32,2304]{1,0:T(8,128)(2,1)S(1)}, bf16[32,2304]{1,0:T(8,128)(2,1)S(1)}, u32[]{:S(2)}, u32[]{:S(2)}) collective-permute-start(bf16[32,2304]{1,0:T(8,128)(2,1)S(1)} %get-tuple-element.31), channel_id=1, source_target_pairs={{0,56},{1,57},{2,58},{3,59},{4,12},{5,13},{6,14},{7,15},{8,0},{9,1... | collective-permute-start | bytes 442376 | tf_op jit(solution)/shard_map/ppermute | solution.py:55
  131.3 13.3 %collective-permute-start.34 = (bf16[32,2304]{1,0:T(8,128)(2,1)S(1)}, bf16[32,2304]{1,0:T(8,128)(2,1)S(1)}, u32[]{:S(2)}, u32[]{:S(2)}) collective-permute-start(bf16[32,2304]{1,0:T(8,128)(2,1)S(1)} %get-tuple-element.32), channel_id=1, source_target_pairs={{0,48},{1,49},{2,50},{3,51},{4,20},{5,21},{6,22},{7,23},{8,56},{9,... | collective-permute-start | bytes 442376 | tf_op jit(solution)/shard_map/ppermute | solution.py:55
  132.2 9.2 %collective-permute-start.36 = (bf16[16,2304]{1,0:T(8,128)(2,1)S(1)}, bf16[16,2304]{1,0:T(8,128)(2,1)S(1)}, u32[]{:S(2)}, u32[]{:S(2)}) collective-permute-start(bf16[16,2304]{1,0:T(8,128)(2,1)S(1)} %get-tuple-element.34), channel_id=1, source_target_pairs={{0,32},{1,33},{2,34},{3,35},{4,36},{5,37},{6,38},{7,39},{8,40},{9,... | collective-permute-start | bytes 221192 | tf_op jit(solution)/shard_map/ppermute | solution.py:55
  141.4 14.9 %collective-permute-start.1 = (bf16[512,256]{1,0:T(8,128)(2,1)S(1)}, bf16[512,256]{1,0:T(8,128)(2,1)S(1)}, u32[]{:S(2)}, u32[]{:S(2)}) collective-permute-start(bf16[512,256]{1,0:T(8,128)(2,1)S(1)} %get-tuple-element.46), channel_id=1, source_target_pairs={{0,1},{1,2},{2,3},{3,0},{4,5},{5,6},{6,7},{7,4},{8,9},{9,10},{10,1... | collective-permute-start | bytes 786440 | tf_op jit(solution)/shard_map/ppermute | solution.py:55
  142.6 19.2 %collective-permute-start.2 = (bf16[512,256]{1,0:T(8,128)(2,1)S(1)}, bf16[512,256]{1,0:T(8,128)(2,1)S(1)}, u32[]{:S(2)}, u32[]{:S(2)}) collective-permute-start(bf16[512,256]{1,0:T(8,128)(2,1)S(1)} %get-tuple-element.46), channel_id=1, source_target_pairs={{0,2},{1,3},{2,0},{3,1},{4,6},{5,7},{6,4},{7,5},{8,10},{9,11},{10,... | collective-permute-start | bytes 786440 | tf_op jit(solution)/shard_map/ppermute | solution.py:55
  144.6 17.2 %collective-permute-start.3 = (bf16[512,256]{1,0:T(8,128)(2,1)S(1)}, bf16[512,256]{1,0:T(8,128)(2,1)S(1)}, u32[]{:S(2)}, u32[]{:S(2)}) collective-permute-start(bf16[512,256]{1,0:T(8,128)(2,1)S(1)} %get-tuple-element.46), channel_id=1, source_target_pairs={{0,3},{1,0},{2,1},{3,2},{4,7},{5,4},{6,5},{7,6},{8,11},{9,8},{10,9... | collective-permute-start | bytes 786440 | tf_op jit(solution)/shard_map/ppermute | solution.py:55
  145.0 8.2 %collective-permute-start.35 = (bf16[32,2304]{1,0:T(8,128)(2,1)S(1)}, bf16[32,2304]{1,0:T(8,128)(2,1)S(1)}, u32[]{:S(2)}, u32[]{:S(2)}) collective-permute-start(bf16[32,2304]{1,0:T(8,128)(2,1)S(1)} %get-tuple-element.33), channel_id=1, source_target_pairs={{0,40},{1,41},{2,42},{3,43},{4,28},{5,29},{6,30},{7,31},{8,48},{9,... | collective-permute-start | bytes 442376 | tf_op jit(solution)/shard_map/ppermute | solution.py:55
  153.2 14.4 %collective-permute-start.12 = (bf16[4,128,256]{2,1,0:T(8,128)(2,1)S(1)}, bf16[4,128,256]{2,1,0:T(8,128)(2,1)S(1)}, u32[]{:S(2)}, u32[]{:S(2)}) collective-permute-start(bf16[4,128,256]{2,1,0:T(8,128)(2,1)S(1)} %fusion), channel_id=1, source_target_pairs={{0,8},{1,9},{2,10},{3,11},{4,60},{5,61},{6,62},{7,63},{8,16},{9,17... | collective-permute-start | bytes 786440 | tf_op jit(solution)/shard_map/ppermute | solution.py:55
  156.4 11.2 %collective-permute-start.37 = (f32[16,2304]{1,0:T(8,128)S(1)}, f32[16,2304]{1,0:T(8,128)S(1)}, u32[]{:S(2)}, u32[]{:S(2)}) collective-permute-start(f32[16,2304]{1,0:T(8,128)S(1)} %get-tuple-element.36), channel_id=1, source_target_pairs={{0,4},{1,5},{2,6},{3,7},{4,0},{5,1},{6,2},{7,3},{8,12},{9,13},{10,... | collective-permute-start | bytes 442376 | tf_op jit(solution)/shard_map/ppermute | solution.py:55
  (17 other events, 62.1 us)
where the time goes:
time: 174 us; the launch traced here: 173 us
  waiting for transfers between devices  78.1 us (45%)
  starting transfers between devices  63.7 us (37%)
  Pallas kernels  22 us (13%)
  other arithmetic  6.23 us (4%)
    ppermute x38, waiting for transfers between devices, routed(): return lax.ppermute(value, ('fsdp', 'tensor'), pairs)  78.1 us
    ppermute x38, starting transfers between devices, routed(): return lax.ppermute(value, ('fsdp', 'tensor'), pairs)  63.7 us
    pallas_call x10, Pallas kernels, call(): pl.pallas_call(body, out_shape=outs, in_specs=([SCALARS] if scalars else...  22 us
  transfers between devices with their start and end apart: 38, of which 15 were waited for; matrix products, arithmetic and copies ran while one was open for 4% of the time, Pallas kernels for 11%

commit v1 on v0

--- a/solution.py
+++ b/solution.py
@@ -124,65 +124,84 @@
     return jnp.concatenate(rows, axis=0)
 
 
-def scores_body(info, slots_ref, x0, x1, d0, d1, a0, a1, a2, a3, out, acc):
-    toks, width = x0.shape
+def pick_rows(info, slots, scores):
     y, c = info[0], info[2]
-    adapters = (a0, a1, a2, a3)
-    for h, (xr, dr) in enumerate(((x0, d0), (x1, d1))):
-        slots = slots_ref[:, h * toks : (h + 1) * toks]
-        acc[1] = dot_nt(jnp.concatenate([a[:, width:] for a in adapters], axis=0), dr[...])
-        acc[0] = jnp.zeros((512, toks), jnp.float32)
+    total = jnp.zeros((16, slots.shape[1]), jnp.float32)
+    for jy in range(NY):
+        for piece in range(8):
+            hit = slots == ((y - jy) & 3) * 16 + block_of(info, c, piece)
+            at = jy * 128 + piece * 16
+            total = total + jnp.where(hit, scores[at : at + 16, :], 0.0)
+    return total
+
+
+def up_scores_body(info, slots_ref, d0, d1, b0, b1, b2, b3, out, turned, acc):
+    toks = d0.shape[0]
+    for h, dr in enumerate((d0, d1)):
+        cols = slice(h * toks, (h + 1) * toks)
+        acc[...] = dot_nt(jnp.concatenate([b[...] for b in (b0, b1, b2, b3)], axis=0), dr[...])
+        total = pick_rows(info, slots_ref[:, cols], acc) * coefficient
+        out[:, cols] = total
+        turned[:, (1 - h) * toks : (2 - h) * toks] = total
+
+
+def scores_body(info, slots_ref, x0, x1, a0, a1, a2, a3, out, turned, acc):
+    toks = x0.shape[0]
+    for h, xr in enumerate((x0, x1)):
+        cols = slice(h * toks, (h + 1) * toks)
+        acc[...] = jnp.zeros_like(acc)
 
         @pl.loop(0, 2)
         def _(k, xr=xr):
             at = pl.ds(pl.multiple_of(k * 1024, 1024), 1024)
-            acc[0] += dot_nt(jnp.concatenate([a[:, at] for a in adapters], axis=0), xr[:, at])
-
-        in_sum = jnp.zeros((16, toks), jnp.float32)
-        grad_sum = jnp.zeros((16, toks), jnp.float32)
-        for jy in range(NY):
-            for piece in range(8):
-                hit = slots == ((y - jy) & 3) * 16 + block_of(info, c, piece)
-                rows = slice(jy * 128 + piece * 16, jy * 128 + piece * 16 + 16)
-                in_sum = in_sum + jnp.where(hit, acc[0, rows, :], 0.0)
-                grad_sum = grad_sum + jnp.where(hit, acc[1, rows, :], 0.0)
-        out[0:16, h * toks : (h + 1) * toks] = in_sum * inverse_width
-        out[16:32, h * toks : (h + 1) * toks] = grad_sum * coefficient
-
-
-def terms_body(info, slots_ref, low_ref, x0, x1, d0, d1, o0, o1, o2, o3, sg, si):
-    toks, width = x0.shape
-    outs = (o0, o1, o2, o3)
+            acc[...] += dot_nt(jnp.concatenate([a[:, at] for a in (a0, a1, a2, a3)], axis=0), xr[:, at])
+
+        total = pick_rows(info, slots_ref[:, cols], acc) * inverse_width
+        out[:, cols] = total
+        turned[:, (1 - h) * toks : (2 - h) * toks] = total
+
+
+def spread_all(info, slots_ref, low_ref, toks, spread):
     for h in range(2):
         cols = slice(h * toks, (h + 1) * toks)
-        slots = slots_ref[:, cols]
         low = low_ref[:, cols].astype(jnp.float32)
         for jy in range(NY):
-            rows = slice(jy * 128, (jy + 1) * 128)
-            sg[h, rows, :] = spread_rows(info, slots, low[16:32], jy).astype(jnp.bfloat16)
-            si[h, rows, :] = spread_rows(info, slots, low[0:16], jy).astype(jnp.bfloat16)
+            rows = spread_rows(info, slots_ref[:, cols], low, jy)
+            spread[h, jy * 128 : (jy + 1) * 128, :] = rows.astype(jnp.bfloat16)
+
+
+def down_terms_body(info, slots_ref, low_ref, x0, x1, o0, o1, o2, o3, spread):
+    toks, width = x0.shape
+    spread_all(info, slots_ref, low_ref, toks, spread)
 
     @pl.loop(0, width // 256)
     def _(k):
         at = pl.ds(pl.multiple_of(k * 256, 256), 256)
-        down = dot_nn(sg[0], x0[:, at]) + dot_nn(sg[1], x1[:, at])
+        down = dot_nn(spread[0], x0[:, at]) + dot_nn(spread[1], x1[:, at])
         down = (down * inverse_width).astype(jnp.bfloat16)
-        for jy, out in enumerate(outs):
+        for jy, out in enumerate((o0, o1, o2, o3)):
             out[:, at] = down[jy * 128 : (jy + 1) * 128]
 
-    up = dot_nn(si[0], d0[...]) + dot_nn(si[1], d1[...])
+
+def up_terms_body(info, slots_ref, low_ref, d0, d1, o0, o1, o2, o3, spread):
+    spread_all(info, slots_ref, low_ref, d0.shape[0], spread)
+    up = dot_nn(spread[0], d0[...]) + dot_nn(spread[1], d1[...])
     up = (up * coefficient).astype(jnp.bfloat16)
-    for jy, out in enumerate(outs):
-        out[:, width:] = up[jy * 128 : (jy + 1) * 128]
-
-
-def y_sums_body(r0, r1, r2, r3, o0, o1, o2, o3, o4):
+    for jy, out in enumerate((o0, o1, o2, o3)):
+        out[...] = up[jy * 128 : (jy + 1) * 128]
+
+
+def y_sums_body(r0, r1, r2, r3, u0, u1, u2, u3, *outs):
+    width = r0.shape[1]
     at = 0
-    for out in (o0, o1, o2, o3, o4):
+    for out in outs:
         rows = slice(at, at + out.shape[0])
         total = r0[rows, :].astype(jnp.float32) + r1[rows, :].astype(jnp.float32)
         total = total + r2[rows, :].astype(jnp.float32) + r3[rows, :].astype(jnp.float32)
-        out[...] = total.astype(out.dtype)
+        out[:, :width] = total.astype(out.dtype)
+        total = u0[rows, :].astype(jnp.float32) + u1[rows, :].astype(jnp.float32)
+        total = total + u2[rows, :].astype(jnp.float32) + u3[rows, :].astype(jnp.float32)
+        out[:, width:] = total.astype(out.dtype)
         at += out.shape[0]
 
 
@@ -204,7 +223,7 @@
     for h in range(2):
         cols = slice(h * toks, (h + 1) * toks)
         slots = slots_ref[:, cols]
-        low = low_ref[16:32, cols].astype(jnp.float32)
+        low = low_ref[:, cols].astype(jnp.float32)
         for jy in range(NY):
             turned = spread_rows(info, slots, low, jy).T
             spread[cols, jy * 128 : (jy + 1) * 128] = turned.astype(jnp.bfloat16)
@@ -317,15 +336,22 @@
         high = jnp.where(first, other, own)
         return jnp.concatenate([low, high], axis=axis)
 
-    ab = jnp.concatenate([factor_down[0], factor_up[0]], axis=1).astype(jnp.bfloat16)
-    chip_ab = in_order(ab, swap_cores(ab))
-    steps = [both_ways_z(chip_ab, k) for k in range(1, 4)]
-    az = jnp.concatenate([ab] + steps + [both_ways_z(ab, 4)], axis=0)
-    adapters = [az] + [along_y(az, j) for j in range(1, NY)]
-
     matches = tenant_ids[:, None] == jnp.arange(tenant_owner.shape[0], dtype=jnp.int32)[None, :]
     slot_own = jnp.sum(jnp.where(matches, tenant_owner[None, :], 0), axis=1)
-    slot_all = jnp.concatenate([slot_own, swap_cores(slot_own)])
+
+    ab = jnp.concatenate([factor_down[0], factor_up[0]], axis=1).astype(jnp.bfloat16)
+    riders = jnp.broadcast_to(slot_own.astype(jnp.bfloat16)[:, None], (seqs, 128))
+    swapped = swap_cores(jnp.concatenate([ab, riders], axis=1))
+    chip_ab = in_order(ab, swapped[:, :wide])
+    slot_other = swapped[:, wide].astype(jnp.int32)
+    steps = [both_ways_z(chip_ab, k) for k in range(1, 4)]
+    steps = [ab] + steps + [both_ways_z(ab, 4)]
+    bz = jnp.concatenate([s[:, width:] for s in steps], axis=0)
+    az = jnp.concatenate([s[:, :width] for s in steps], axis=0)
+    ups = [bz] + [along_y(bz, j) for j in range(1, NY)]
+    downs = [az] + [along_y(az, j) for j in range(1, NY)]
+
+    slot_all = jnp.concatenate([slot_own, slot_other])
     slots = jnp.broadcast_to(slot_all[:, None], (2 * seqs, seq_len)).reshape(1, 2 * toks)
     live_tok = jnp.arange(toks, dtype=jnp.int32) // seq_len < live_counts[0]
     d0 = jnp.where(live_tok[:, None], value_grad, jnp.zeros_like(value_grad))
@@ -352,29 +378,39 @@
 
     b01, b2, b3 = base(w0, w1), base(w2), base(w3)
 
-    part = call(
-        scores_body,
-        (info, slots, x0, x1, d0, d1, *adapters),
-        [shape_of((32, 2 * toks), jnp.float32)],
-        2 * 2 * toks * 512 * wide,
-        scratch=[pltpu.VMEM((2, 512, toks), jnp.float32)],
-    )[0]
-    pair = part[:, :toks] + swap_cores(part[:, toks:])
-    low = pair
-    for j in range(1, NX):
-        low = low + along_x(pair, j)
-    low = low.astype(jnp.bfloat16)
-    low = jnp.concatenate([low, swap_cores(low)], axis=1)
+    def rank_sums(body, operands, flops):
+        own, turned = call(
+            body,
+            operands,
+            [shape_of((ADAPTER_RANK, 2 * toks), jnp.float32)] * 2,
+            flops,
+            scratch=[pltpu.VMEM((512, toks), jnp.float32)],
+        )
+        pair = own + swap_cores(turned)
+        total = pair
+        for j in range(1, NX):
+            total = total + along_x(pair, j)
+        return total.astype(jnp.bfloat16)
 
     spread = pltpu.VMEM((2, 512, toks), jnp.bfloat16)
-    terms = call(
-        terms_body,
-        (info, slots, low, x0, x1, d0, d1),
-        [shape_of((128, wide), jnp.bfloat16)] * NY,
-        2 * 2 * toks * 512 * wide,
-        scratch=[spread, spread],
-    )
+    rank_flops = 2 * 2 * toks * 512
+
+    def row_terms(body, operands, columns):
+        return call(
+            body,
+            operands,
+            [shape_of((128, columns), jnp.bfloat16)] * NY,
+            rank_flops * columns,
+            scratch=[spread],
+        )
+
+    low = rank_sums(up_scores_body, (info, slots, d0, d1, *ups), rank_flops * values)
+    terms = row_terms(down_terms_body, (info, slots, low, x0, x1), width)
     arrived = [terms[0]] + [along_y(terms[j], -j) for j in range(1, NY)]
+
+    in_low = rank_sums(scores_body, (info, slots, x0, x1, *downs), rank_flops * width)
+    terms = row_terms(up_terms_body, (info, slots, in_low, d0, d1), values)
+    arrived += [terms[0]] + [along_y(terms[j], -j) for j in range(1, NY)]
     pieces = call(
         y_sums_body,
         tuple(arrived),
@@ -400,7 +436,7 @@
 
     keep, send = call(
         back_body,
-        (info, slots, low, *adapters),
+        (info, slots, low, *downs),
         [shape_of((2 * toks, half), jnp.bfloat16)] * 2,
         2 * 2 * toks * 512 * width,
         scratch=[

time: 174 us -> 173 us (level)
  waiting for transfers between devices: 78.1 us -> 70.3 us
  starting transfers between devices: 63.7 us -> 70.7 us
  other arithmetic: 6.23 us -> 4.48 us
    ppermute x38 -> x46, waiting for transfers between devices: 78.1 us -> 70.3 us  [routed(): return lax.ppermute(value, ('fsdp', 'tensor'), pairs)]
    ppermute x38 -> x46, starting transfers between devices: 63.7 us -> 70.7 us  [routed(): return lax.ppermute(value, ('fsdp', 'tensor'), pairs)]
    pallas_call x10 -> x12, Pallas kernels: 22 us -> 22.9 us  [call(): pl.pallas_call(body, out_shape=outs, in_specs=([SCALARS] if scalars else...]
  transfers between devices with their start and end apart: 38 -> 46, of which waited for: 15 -> 11; matrix products, arithmetic and copies ran while one was open for 4% -> 2% of each run, Pallas kernels for 11% -> 11%
where the time goes in v1:
time: 173 us; the launch traced here: 172 us
  starting transfers between devices  70.7 us (41%)
  waiting for transfers between devices  70.3 us (41%)
  Pallas kernels  22.9 us (13%)
  other arithmetic  4.48 us (3%)
  local copies, waits for them, and re-layouts  1.88 us (1%)
  between operations  1.8 us (1%)
    ppermute x46, starting transfers between devices, routed(): return lax.ppermute(value, ('fsdp', 'tensor'), pairs)  70.7 us
    ppermute x46, waiting for transfers between devices, routed(): return lax.ppermute(value, ('fsdp', 'tensor'), pairs)  70.3 us
    pallas_call x12, Pallas kernels, call(): pl.pallas_call(body, out_shape=outs, in_specs=([SCALARS] if scalars else...  22.9 us
  transfers between devices with their start and end apart: 46, of which 11 were waited for; matrix products, arithmetic and copies ran while one was open for 2% of the time, Pallas kernels for 11%

profile of v1, /device:TPU:1, one launch (start us, length us, event | category | flops | bytes accessed | tf_op | source)
XLA Modules:
  0.0 172.0 jit_solution(16359114394611026571)
XLA Ops:
  2.5 3.3 %collective-permute-start.13 = (bf16[16,2432]{1,0:T(8,128)(2,1)S(1)}, bf16[16,2432]{1,0:T(8,128)(2,1)S(1)}, u32[]{:S(2)}, u32[]{:S(2)}) collective-permute-start(bf16[16,2432]{1,0:T(8,128)(2,1)S(1)} %pad_maximum_fusion.5), channel_id=1, source_target_pairs={{0,4},{1,5},{2,6},{3,7},{4,0},{5,1},{6,2},{7,3},{8,12},{9,13},{10,... | collective-permute-start | bytes 233480 | tf_op jit(solution)/shard_map/ppermute | solution.py:55
  8.4 4.1 %collective-permute-start.5 = (bf16[128,256]{1,0:T(8,128)(2,1)S(1)}, bf16[128,256]{1,0:T(8,128)(2,1)S(1)}, u32[]{:S(2)}, u32[]{:S(2)}) collective-permute-start(bf16[128,256]{1,0:T(8,128)(2,1)S(1)} %collective-permute-done.4), channel_id=1, source_target_pairs={{0,64},{1,65},{2,66},{3,67},{4,68},{5,69},{6,70},{7,71},{8,72},{9,... | collective-permute-start | bytes 196616 | tf_op jit(solution)/shard_map/ppermute | solution.py:55
  12.5 6.9 %collective-permute-start.6 = (bf16[128,256]{1,0:T(8,128)(2,1)S(1)}, bf16[128,256]{1,0:T(8,128)(2,1)S(1)}, u32[]{:S(2)}, u32[]{:S(2)}) collective-permute-start(bf16[128,256]{1,0:T(8,128)(2,1)S(1)} %collective-permute-done.4), channel_id=1, source_target_pairs={{0,128},{1,129},{2,130},{3,131},{4,132},{5,133},{6,134},{7,135},{8... | collective-permute-start | bytes 196616 | tf_op jit(solution)/shard_map/ppermute | solution.py:55
  19.4 5.7 %collective-permute-start.14 = (bf16[32,2304]{1,0:T(8,128)(2,1)S(1)}, bf16[32,2304]{1,0:T(8,128)(2,1)S(1)}, u32[]{:S(2)}, u32[]{:S(2)}) collective-permute-start(bf16[32,2304]{1,0:T(8,128)(2,1)S(1)} %pad_maximum_fusion.4), channel_id=1, source_target_pairs={{0,8},{1,9},{2,10},{3,11},{4,60},{5,61},{6,62},{7,63},{8,16},{9,17... | collective-permute-start | bytes 442376 | tf_op jit(solution)/shard_map/ppermute | solution.py:55
  25.3 3.7 %collective-permute-start.15 = (bf16[32,2304]{1,0:T(8,128)(2,1)S(1)}, bf16[32,2304]{1,0:T(8,128)(2,1)S(1)}, u32[]{:S(2)}, u32[]{:S(2)}) collective-permute-start(bf16[32,2304]{1,0:T(8,128)(2,1)S(1)} %pad_maximum_fusion.4), channel_id=1, source_target_pairs={{0,16},{1,17},{2,18},{3,19},{4,52},{5,53},{6,54},{7,55},{8,24},{9,... | collective-permute-start | bytes 442376 | tf_op jit(solution)/shard_map/ppermute | solution.py:55
  29.1 2.8 %collective-permute-start.16 = (bf16[32,2304]{1,0:T(8,128)(2,1)S(1)}, bf16[32,2304]{1,0:T(8,128)(2,1)S(1)}, u32[]{:S(2)}, u32[]{:S(2)}) collective-permute-start(bf16[32,2304]{1,0:T(8,128)(2,1)S(1)} %pad_maximum_fusion.4), channel_id=1, source_target_pairs={{0,24},{1,25},{2,26},{3,27},{4,44},{5,45},{6,46},{7,47},{8,32},{9,... | collective-permute-start | bytes 442376 | tf_op jit(solution)/shard_map/ppermute | solution.py:55
  31.9 2.0 %collective-permute-start.17 = (bf16[16,2304]{1,0:T(8,128)(2,1)S(1)}, bf16[16,2304]{1,0:T(8,128)(2,1)S(1)}, u32[]{:S(2)}, u32[]{:S(2)}) collective-permute-start(bf16[16,2304]{1,0:T(8,128)(2,1)S(1)} %get-tuple-element.69), channel_id=1, source_target_pairs={{0,32},{1,33},{2,34},{3,35},{4,36},{5,37},{6,38},{7,39},{8,40},{9,... | collective-permute-start | bytes 221192 | tf_op jit(solution)/shard_map/ppermute | solution.py:55
  35.4 5.3 %collective-permute-done.16 = bf16[32,2304]{1,0:T(8,128)(2,1)S(1)} collective-permute-done((bf16[32,2304]{1,0:T(8,128)(2,1)S(1)}, bf16[32,2304]{1,0:T(8,128)(2,1)S(1)}, u32[]{:S(2)}, u32[]{:S(2)}) %collective-permute-start.16) | collective-permute-done | bytes 147488 | tf_op jit(solution)/shard_map/ppermute | solution.py:55
  40.6 1.5 collective-permute-done.17
  42.9 2.7 %collective-permute-start.25 = (bf16[128,2048]{1,0:T(8,128)(2,1)S(1)}, bf16[128,2048]{1,0:T(8,128)(2,1)}, u32[]{:S(2)}, u32[]{:S(2)}) collective-permute-start(bf16[128,2048]{1,0:T(8,128)(2,1)S(1)} %slice_dynamic-update-slice_fusion.3.a0), channel_id=1, source_target_pairs={{0,64},{1,65},{2,66},{3,67},{4,68},{5,69},{6,70},{7,71},{8,72},{9,... | collective-permute-start | bytes 1572872 | tf_op jit(solution)/shard_map/ppermute | solution.py:55
  46.7 1.5 collective-permute-start.27
  50.3 20.8 %collective-permute-done.20.b3 = bf16[128,256]{1,0:T(8,128)(2,1)S(1)} collective-permute-done((bf16[128,256]{1,0:T(8,128)(2,1)S(1)}, bf16[128,256]{1,0:T(8,128)(2,1)S(1)}, u32[]{:S(2)}, u32[]{:S(2)}) %collective-permute-start.20) | collective-permute-done | bytes 65568 | tf_op jit(solution)/shard_map/ppermute | solution.py:55
  73.1 3.8 %collective-permute-start.21 = (f32[16,512]{1,0:T(8,128)S(1)}, f32[16,512]{1,0:T(8,128)S(1)}, u32[]{:S(2)}, u32[]{:S(2)}) collective-permute-start(f32[16,512]{1,0:T(8,128)S(1)} %get-tuple-element.31), channel_id=1, source_target_pairs={{0,4},{1,5},{2,6},{3,7},{4,0},{5,1},{6,2},{7,3},{8,12},{9,13},{10,... | collective-permute-start | bytes 98312 | tf_op jit(solution)/shard_map/ppermute | solution.py:55
  76.9 3.5 %shard_map.206 = (f32[16,512]{1,0:T(8,128)S(1)}, f32[16,512]{1,0:T(8,128)S(1)}) custom-call(s32[4]{0:T(128)S(1)} %and_select_fusion.1.info, s32[1,512]{1,0:T(1,128)S(1)} %reshape.53.slots_ref, bf16[256,2048]{1,0:T(8,128)(2,1)S(1)} %copy-done, bf16[256,2048]{1,0:T(8,128)(2,1)S(1)} %collective-permute-done.30.x1, ...), custom_call_target="tpu_custom_call" | custom-call | flops 1073741824 | bytes 4261904 | tf_op jit(solution)/shard_map/pallas_call | solution.py:298
  81.2 2.5 %collective-permute-start.23 = (f32[16,512]{1,0:T(8,128)S(1)}, f32[16,512]{1,0:T(8,128)S(1)}, u32[]{:S(2)}, u32[]{:S(2)}) collective-permute-start(f32[16,512]{1,0:T(8,128)S(1)} %add.78), channel_id=1, source_target_pairs={{0,2},{1,3},{2,0},{3,1},{4,6},{5,7},{6,4},{7,5},{8,10},{9,11},{10,... | collective-permute-start | bytes 98312 | tf_op jit(solution)/shard_map/ppermute | solution.py:55
  86.2 1.9 %collective-permute-start.37 = (f32[16,512]{1,0:T(8,128)S(1)}, f32[16,512]{1,0:T(8,128)S(1)}, u32[]{:S(2)}, u32[]{:S(2)}) collective-permute-start(f32[16,512]{1,0:T(8,128)S(1)} %add.82), channel_id=1, source_target_pairs={{0,3},{1,0},{2,1},{3,2},{4,7},{5,4},{6,5},{7,6},{8,11},{9,8},{10,9... | collective-permute-start | bytes 98312 | tf_op jit(solution)/shard_map/ppermute | solution.py:55
  90.8 2.4 %collective-permute-start.38 = (bf16[128,256]{1,0:T(8,128)(2,1)S(1)}, bf16[128,256]{1,0:T(8,128)(2,1)S(1)}, u32[]{:S(2)}, u32[]{:S(2)}) collective-permute-start(bf16[128,256]{1,0:T(8,128)(2,1)S(1)} %get-tuple-element.43), channel_id=1, source_target_pairs={{0,192},{1,193},{2,194},{3,195},{4,196},{5,197},{6,198},{7,199},{8... | collective-permute-start | bytes 196616 | tf_op jit(solution)/shard_map/ppermute | solution.py:55
  94.4 3.1 %shard_map.205 = (bf16[128,2048]{1,0:T(8,128)(2,1)S(1)}, bf16[128,2048]{1,0:T(8,128)(2,1)S(1)}, bf16[128,2048]{1,0:T(8,128)(2,1)S(1)}, bf16[128,2048]{1,0:T(8,128)(2,1)S(1)}) custom-call(s32[4]{0:T(128)S(1)} %and_select_fusion.1.info, s32[1,512]{1,0:T(1,128)S(1)} %reshape.53.slots_ref, bf16[16,512]{1,0:T(8,128)(2,1)S(1)} %add_convert_fusion.1.low_ref, ...), custom_call_target="tpu_custom_call" | custom-call | flops 1073741824 | bytes 4212752 | tf_op jit(solution)/shard_map/pallas_call | solution.py:298
  101.0 4.4 %shard_map.202 = (bf16[512,1024]{1,0:T(8,128)(2,1)S(1)}, bf16[512,1024]{1,0:T(8,128)(2,1)S(1)}) custom-call(s32[4]{0:T(128)S(1)} %and_select_fusion.1.info, s32[1,512]{1,0:T(1,128)S(1)} %reshape.53.slots_ref, bf16[16,512]{1,0:T(8,128)(2,1)S(1)} %add_convert_fusion.1.low_ref, bf16[128,2048]{1,0:T(8,128)(2,1)S(1)} %slice_dynamic-update-slice_fusion.3.a0, ...), custom_call_target="tpu_custom_call" | custom-call | flops 1073741824 | bytes 4212752 | tf_op jit(solution)/shard_map/pallas_call | solution.py:298
  105.4 20.9 %collective-permute-done.40.u3 = bf16[128,256]{1,0:T(8,128)(2,1)S(1)} collective-permute-done((bf16[128,256]{1,0:T(8,128)(2,1)S(1)}, bf16[128,256]{1,0:T(8,128)(2,1)S(1)}, u32[]{:S(2)}, u32[]{:S(2)}) %collective-permute-start.40) | collective-permute-done | bytes 65568 | tf_op jit(solution)/shard_map/ppermute | solution.py:55
  126.8 1.7 %collective-permute-start.11 = (bf16[2,4,128,256]{3,2,1,0:T(8,128)(2,1)S(1)}, bf16[2,4,128,256]{3,2,1,0:T(8,128)(2,1)S(1)}, u32[]{:S(2)}, u32[]{:S(2)}) collective-permute-start(bf16[2,4,128,256]{3,2,1,0:T(8,128)(2,1)S(1)} %collective-permute-done.10.refs_0_), channel_id=1, source_target_pairs={{0,8},{1,9},{2,10},{3,11},{4,60},{5,61},{6,62},{7,63},{8,16},{9,17... | collective-permute-start | bytes 1572872 | tf_op jit(solution)/shard_map/ppermute | solution.py:55
  128.9 1.3 collective-permute-start.42
  130.3 3.0 %collective-permute-start.44 = (bf16[16,2304]{1,0:T(8,128)(2,1)S(1)}, bf16[16,2304]{1,0:T(8,128)(2,1)S(1)}, u32[]{:S(2)}, u32[]{:S(2)}) collective-permute-start(bf16[16,2304]{1,0:T(8,128)(2,1)S(1)} %get-tuple-element.50), channel_id=1, source_target_pairs={{0,32},{1,33},{2,34},{3,35},{4,36},{5,37},{6,38},{7,39},{8,40},{9,... | collective-permute-start | bytes 221192 | tf_op jit(solution)/shard_map/ppermute | solution.py:55
  133.3 10.9 %collective-permute-done.44.r4 = bf16[16,2304]{1,0:T(8,128)(2,1)S(1)} collective-permute-done((bf16[16,2304]{1,0:T(8,128)(2,1)S(1)}, bf16[16,2304]{1,0:T(8,128)(2,1)S(1)}, u32[]{:S(2)}, u32[]{:S(2)}) %collective-permute-start.44) | collective-permute-done | bytes 73760 | tf_op jit(solution)/shard_map/ppermute | solution.py:55
  144.2 3.7 %collective-permute-start.2 = (bf16[512,256]{1,0:T(8,128)(2,1)S(1)}, bf16[512,256]{1,0:T(8,128)(2,1)S(1)}, u32[]{:S(2)}, u32[]{:S(2)}) collective-permute-start(bf16[512,256]{1,0:T(8,128)(2,1)S(1)} %get-tuple-element.66), channel_id=1, source_target_pairs={{0,2},{1,3},{2,0},{3,1},{4,6},{5,7},{6,4},{7,5},{8,10},{9,11},{10,... | collective-permute-start | bytes 786440 | tf_op jit(solution)/shard_map/ppermute | solution.py:55
  148.1 8.6 %collective-permute-done.43.r3 = bf16[32,2304]{1,0:T(8,128)(2,1)S(1)} collective-permute-done((bf16[32,2304]{1,0:T(8,128)(2,1)S(1)}, bf16[32,2304]{1,0:T(8,128)(2,1)S(1)}, u32[]{:S(2)}, u32[]{:S(2)}) %collective-permute-start.43) | collective-permute-done | bytes 147488 | tf_op jit(solution)/shard_map/ppermute | solution.py:55
  157.3 3.2 %collective-permute-start.45 = (f32[16,2304]{1,0:T(8,128)S(1)}, f32[16,2304]{1,0:T(8,128)S(1)}, u32[]{:S(2)}, u32[]{:S(2)}) collective-permute-start(f32[16,2304]{1,0:T(8,128)S(1)} %get-tuple-element.52), channel_id=1, source_target_pairs={{0,4},{1,5},{2,6},{3,7},{4,0},{5,1},{6,2},{7,3},{8,12},{9,13},{10,... | collective-permute-start | bytes 442376 | tf_op jit(solution)/shard_map/ppermute | solution.py:55
  160.7 2.3 %shard_map.198.b01 = f32[512,384]{1,0:T(8,128)S(1)} custom-call(s32[4]{0:T(128)S(1)} %and_select_fusion.1.info, bf16[4,512,256]{2,1,0:T(8,128)(2,1)S(1)} %pad_maximum_fusion.dv, bf16[4,128,256]{2,1,0:T(8,128)(2,1)S(1)} %pad_maximum_fusion.3.refs_0_, bf16[2,4,128,256]{3,2,1,0:T(8,128)(2,1)} %collective-permute-done.9.refs_1_), custom_call_target="tpu_custom_call" | custom-call | flops 402653184 | bytes 2621456 | tf_op jit(solution)/shard_map/pallas_call | solution.py:298
  163.0 1.6 shard_map.199.b2
  164.7 1.6 shard_map.200.b3
  166.4 1.8 %shard_map.203 = (bf16[256,1024]{1,0:T(8,128)(2,1)S(1)}, bf16[256,1024]{1,0:T(8,128)(2,1)S(1)}) custom-call(s32[4]{0:T(128)S(1)} %and_select_fusion.1.info, bf16[4,512,256]{2,1,0:T(8,128)(2,1)S(1)} %pad_maximum_fusion.dv, bf16[4,128,256]{2,1,0:T(8,128)(2,1)S(1)} %collective-permute-done.12.w4, f32[512,384]{1,0:T(8,128)S(1)} %shard_map.198.b01, ...), custom_call_target="tpu_custom_call" | custom-call | flops 134217728 | bytes 6291472 | tf_op jit(solution)/shard_map/pallas_call | solution.py:298
  170.2 1.8 %shard_map.204 = bf16[256,2048]{1,0:T(8,128)(2,1)} custom-call(s32[4]{0:T(128)S(1)} %and_select_fusion.1.info, bf16[256,1024]{1,0:T(8,128)(2,1)S(1)} %get-tuple-element.34.own, bf16[256,1024]{1,0:T(8,128)(2,1)S(1)} %collective-permute-done.29.other), custom_call_target="tpu_custom_call" | custom-call | bytes 2097168 | tf_op jit(solution)/shard_map/pallas_call | solution.py:298
  (139 shorter events, 25.7 us)
Async XLA Ops:
  2.5 16.8 %collective-permute-start.13 = (bf16[16,2432]{1,0:T(8,128)(2,1)S(1)}, bf16[16,2432]{1,0:T(8,128)(2,1)S(1)}, u32[]{:S(2)}, u32[]{:S(2)}) collective-permute-start(bf16[16,2432]{1,0:T(8,128)(2,1)S(1)} %pad_maximum_fusion.5), channel_id=1, source_target_pairs={{0,4},{1,5},{2,6},{3,7},{4,0},{5,1},{6,2},{7,3},{8,12},{9,13},{10,... | collective-permute-start | bytes 233480 | tf_op jit(solution)/shard_map/ppermute | solution.py:55
  5.8 71.1 %collective-permute-start.30 = (bf16[256,2048]{1,0:T(8,128)(2,1)}, bf16[256,2048]{1,0:T(8,128)(2,1)S(1)}, u32[]{:S(2)}, u32[]{:S(2)}) collective-permute-start(bf16[256,2048]{1,0:T(8,128)(2,1)} %x0.3), channel_id=1, source_target_pairs={{0,4},{1,5},{2,6},{3,7},{4,0},{5,1},{6,2},{7,3},{8,12},{9,13},{10,... | collective-permute-start | bytes 3145736 | tf_op jit(solution)/shard_map/ppermute | solution.py:55
  8.4 16.8 %collective-permute-start.5 = (bf16[128,256]{1,0:T(8,128)(2,1)S(1)}, bf16[128,256]{1,0:T(8,128)(2,1)S(1)}, u32[]{:S(2)}, u32[]{:S(2)}) collective-permute-start(bf16[128,256]{1,0:T(8,128)(2,1)S(1)} %collective-permute-done.4), channel_id=1, source_target_pairs={{0,64},{1,65},{2,66},{3,67},{4,68},{5,69},{6,70},{7,71},{8,72},{9,... | collective-permute-start | bytes 196616 | tf_op jit(solution)/shard_map/ppermute | solution.py:55
  12.5 12.8 %collective-permute-start.6 = (bf16[128,256]{1,0:T(8,128)(2,1)S(1)}, bf16[128,256]{1,0:T(8,128)(2,1)S(1)}, u32[]{:S(2)}, u32[]{:S(2)}) collective-permute-start(bf16[128,256]{1,0:T(8,128)(2,1)S(1)} %collective-permute-done.4), channel_id=1, source_target_pairs={{0,128},{1,129},{2,130},{3,131},{4,132},{5,133},{6,134},{7,135},{8... | collective-permute-start | bytes 196616 | tf_op jit(solution)/shard_map/ppermute | solution.py:55
  19.4 9.7 %collective-permute-start.7 = (bf16[128,256]{1,0:T(8,128)(2,1)S(1)}, bf16[128,256]{1,0:T(8,128)(2,1)S(1)}, u32[]{:S(2)}, u32[]{:S(2)}) collective-permute-start(bf16[128,256]{1,0:T(8,128)(2,1)S(1)} %collective-permute-done.4), channel_id=1, source_target_pairs={{0,192},{1,193},{2,194},{3,195},{4,196},{5,197},{6,198},{7,199},{8... | collective-permute-start | bytes 196616 | tf_op jit(solution)/shard_map/ppermute | solution.py:55
  19.4 12.5 %collective-permute-start.14 = (bf16[32,2304]{1,0:T(8,128)(2,1)S(1)}, bf16[32,2304]{1,0:T(8,128)(2,1)S(1)}, u32[]{:S(2)}, u32[]{:S(2)}) collective-permute-start(bf16[32,2304]{1,0:T(8,128)(2,1)S(1)} %pad_maximum_fusion.4), channel_id=1, source_target_pairs={{0,8},{1,9},{2,10},{3,11},{4,60},{5,61},{6,62},{7,63},{8,16},{9,17... | collective-permute-start | bytes 442376 | tf_op jit(solution)/shard_map/ppermute | solution.py:55
  25.2 20.4 %collective-permute-start = (bf16[256,256]{1,0:T(8,128)(2,1)S(1)}, bf16[256,256]{1,0:T(8,128)(2,1)S(1)}, u32[]{:S(2)}, u32[]{:S(2)}) collective-permute-start(bf16[256,256]{1,0:T(8,128)(2,1)S(1)} %broadcast_select_fusion.d0), channel_id=1, source_target_pairs={{0,4},{1,5},{2,6},{3,7},{4,0},{5,1},{6,2},{7,3},{8,12},{9,13},{10,... | collective-permute-start | bytes 393224 | tf_op jit(solution)/shard_map/ppermute | solution.py:55
  25.3 8.9 %collective-permute-start.15 = (bf16[32,2304]{1,0:T(8,128)(2,1)S(1)}, bf16[32,2304]{1,0:T(8,128)(2,1)S(1)}, u32[]{:S(2)}, u32[]{:S(2)}) collective-permute-start(bf16[32,2304]{1,0:T(8,128)(2,1)S(1)} %pad_maximum_fusion.4), channel_id=1, source_target_pairs={{0,16},{1,17},{2,18},{3,19},{4,52},{5,53},{6,54},{7,55},{8,24},{9,... | collective-permute-start | bytes 442376 | tf_op jit(solution)/shard_map/ppermute | solution.py:55
  29.1 11.6 %collective-permute-start.16 = (bf16[32,2304]{1,0:T(8,128)(2,1)S(1)}, bf16[32,2304]{1,0:T(8,128)(2,1)S(1)}, u32[]{:S(2)}, u32[]{:S(2)}) collective-permute-start(bf16[32,2304]{1,0:T(8,128)(2,1)S(1)} %pad_maximum_fusion.4), channel_id=1, source_target_pairs={{0,24},{1,25},{2,26},{3,27},{4,44},{5,45},{6,46},{7,47},{8,32},{9,... | collective-permute-start | bytes 442376 | tf_op jit(solution)/shard_map/ppermute | solution.py:55
  31.9 10.2 %collective-permute-start.17 = (bf16[16,2304]{1,0:T(8,128)(2,1)S(1)}, bf16[16,2304]{1,0:T(8,128)(2,1)S(1)}, u32[]{:S(2)}, u32[]{:S(2)}) collective-permute-start(bf16[16,2304]{1,0:T(8,128)(2,1)S(1)} %get-tuple-element.69), channel_id=1, source_target_pairs={{0,32},{1,33},{2,34},{3,35},{4,36},{5,37},{6,38},{7,39},{8,40},{9,... | collective-permute-start | bytes 221192 | tf_op jit(solution)/shard_map/ppermute | solution.py:55
  34.2 8.7 %collective-permute-start.8 = (bf16[4,128,256]{2,1,0:T(8,128)(2,1)S(1)}, bf16[4,128,256]{2,1,0:T(8,128)(2,1)S(1)}, u32[]{:S(2)}, u32[]{:S(2)}) collective-permute-start(bf16[4,128,256]{2,1,0:T(8,128)(2,1)S(1)} %pad_maximum_fusion.3.refs_0_), channel_id=1, source_target_pairs={{0,4},{1,5},{2,6},{3,7},{4,0},{5,1},{6,2},{7,3},{8,12},{9,13},{10,... | collective-permute-start | bytes 786440 | tf_op jit(solution)/shard_map/ppermute | solution.py:55
  42.9 30.2 %collective-permute-start.25 = (bf16[128,2048]{1,0:T(8,128)(2,1)S(1)}, bf16[128,2048]{1,0:T(8,128)(2,1)}, u32[]{:S(2)}, u32[]{:S(2)}) collective-permute-start(bf16[128,2048]{1,0:T(8,128)(2,1)S(1)} %slice_dynamic-update-slice_fusion.3.a0), channel_id=1, source_target_pairs={{0,64},{1,65},{2,66},{3,67},{4,68},{5,69},{6,70},{7,71},{8,72},{9,... | collective-permute-start | bytes 1572872 | tf_op jit(solution)/shard_map/ppermute | solution.py:55
  45.6 31.2 %collective-permute-start.26 = (bf16[128,2048]{1,0:T(8,128)(2,1)S(1)}, bf16[128,2048]{1,0:T(8,128)(2,1)}, u32[]{:S(2)}, u32[]{:S(2)}) collective-permute-start(bf16[128,2048]{1,0:T(8,128)(2,1)S(1)} %slice_dynamic-update-slice_fusion.3.a0), channel_id=1, source_target_pairs={{0,128},{1,129},{2,130},{3,131},{4,132},{5,133},{6,134},{7,135},{8... | collective-permute-start | bytes 1572872 | tf_op jit(solution)/shard_map/ppermute | solution.py:55
  46.7 30.2 %collective-permute-start.27 = (bf16[128,2048]{1,0:T(8,128)(2,1)S(1)}, bf16[128,2048]{1,0:T(8,128)(2,1)}, u32[]{:S(2)}, u32[]{:S(2)}) collective-permute-start(bf16[128,2048]{1,0:T(8,128)(2,1)S(1)} %slice_dynamic-update-slice_fusion.3.a0), channel_id=1, source_target_pairs={{0,192},{1,193},{2,194},{3,195},{4,196},{5,197},{6,198},{7,199},{8... | collective-permute-start | bytes 1572872 | tf_op jit(solution)/shard_map/ppermute | solution.py:55
  48.2 22.9 %collective-permute-start.20 = (bf16[128,256]{1,0:T(8,128)(2,1)S(1)}, bf16[128,256]{1,0:T(8,128)(2,1)S(1)}, u32[]{:S(2)}, u32[]{:S(2)}) collective-permute-start(bf16[128,256]{1,0:T(8,128)(2,1)S(1)} %constant_dynamic-update-slice_fusion.b0), channel_id=1, source_target_pairs={{0,192},{1,193},{2,194},{3,195},{4,196},{5,197},{6,198},{7,199},{8... | collective-permute-start | bytes 196616 | tf_op jit(solution)/shard_map/ppermute | solution.py:55
  71.1 13.6 %collective-permute-start.9 = (bf16[2,4,128,256]{3,2,1,0:T(8,128)(2,1)}, bf16[2,4,128,256]{3,2,1,0:T(8,128)(2,1)}, u32[]{:S(2)}, u32[]{:S(2)}) collective-permute-start(bf16[2,4,128,256]{3,2,1,0:T(8,128)(2,1)} %pad_maximum_fusion.1), channel_id=1, source_target_pairs={{0,8},{1,9},{2,10},{3,11},{4,60},{5,61},{6,62},{7,63},{8,16},{9,17... | collective-permute-start | bytes 1572872 | tf_op jit(solution)/shard_map/ppermute | solution.py:55
  84.7 42.1 %collective-permute-start.10 = (bf16[2,4,128,256]{3,2,1,0:T(8,128)(2,1)}, bf16[2,4,128,256]{3,2,1,0:T(8,128)(2,1)S(1)}, u32[]{:S(2)}, u32[]{:S(2)}) collective-permute-start(bf16[2,4,128,256]{3,2,1,0:T(8,128)(2,1)} %collective-permute-done.9.refs_1_), channel_id=1, source_target_pairs={{0,8},{1,9},{2,10},{3,11},{4,60},{5,61},{6,62},{7,63},{8,16},{9,17... | collective-permute-start | bytes 1572872 | tf_op jit(solution)/shard_map/ppermute | solution.py:55
  90.8 8.7 %collective-permute-start.38 = (bf16[128,256]{1,0:T(8,128)(2,1)S(1)}, bf16[128,256]{1,0:T(8,128)(2,1)S(1)}, u32[]{:S(2)}, u32[]{:S(2)}) collective-permute-start(bf16[128,256]{1,0:T(8,128)(2,1)S(1)} %get-tuple-element.43), channel_id=1, source_target_pairs={{0,192},{1,193},{2,194},{3,195},{4,196},{5,197},{6,198},{7,199},{8... | collective-permute-start | bytes 196616 | tf_op jit(solution)/shard_map/ppermute | solution.py:55
  97.5 31.0 %collective-permute-start.31 = (bf16[128,2048]{1,0:T(8,128)(2,1)S(1)}, bf16[128,2048]{1,0:T(8,128)(2,1)S(1)}, u32[]{:S(2)}, u32[]{:S(2)}) collective-permute-start(bf16[128,2048]{1,0:T(8,128)(2,1)S(1)} %get-tuple-element.37), channel_id=1, source_target_pairs={{0,192},{1,193},{2,194},{3,195},{4,196},{5,197},{6,198},{7,199},{8... | collective-permute-start | bytes 1572872 | tf_op jit(solution)/shard_map/ppermute | solution.py:55
  98.3 30.2 %collective-permute-start.32 = (bf16[128,2048]{1,0:T(8,128)(2,1)S(1)}, bf16[128,2048]{1,0:T(8,128)(2,1)S(1)}, u32[]{:S(2)}, u32[]{:S(2)}) collective-permute-start(bf16[128,2048]{1,0:T(8,128)(2,1)S(1)} %get-tuple-element.38), channel_id=1, source_target_pairs={{0,128},{1,129},{2,130},{3,131},{4,132},{5,133},{6,134},{7,135},{8... | collective-permute-start | bytes 1572872 | tf_op jit(solution)/shard_map/ppermute | solution.py:55
  99.5 29.0 %collective-permute-start.33 = (bf16[128,2048]{1,0:T(8,128)(2,1)S(1)}, bf16[128,2048]{1,0:T(8,128)(2,1)S(1)}, u32[]{:S(2)}, u32[]{:S(2)}) collective-permute-start(bf16[128,2048]{1,0:T(8,128)(2,1)S(1)} %get-tuple-element.39), channel_id=1, source_target_pairs={{0,64},{1,65},{2,66},{3,67},{4,68},{5,69},{6,70},{7,71},{8,72},{9,... | collective-permute-start | bytes 1572872 | tf_op jit(solution)/shard_map/ppermute | solution.py:55
  100.3 26.0 %collective-permute-start.40 = (bf16[128,256]{1,0:T(8,128)(2,1)S(1)}, bf16[128,256]{1,0:T(8,128)(2,1)S(1)}, u32[]{:S(2)}, u32[]{:S(2)}) collective-permute-start(bf16[128,256]{1,0:T(8,128)(2,1)S(1)} %get-tuple-element.45), channel_id=1, source_target_pairs={{0,64},{1,65},{2,66},{3,67},{4,68},{5,69},{6,70},{7,71},{8,72},{9,... | collective-permute-start | bytes 196616 | tf_op jit(solution)/shard_map/ppermute | solution.py:55
  126.3 40.1 %collective-permute-start.28 = (bf16[512,1024]{1,0:T(8,128)(2,1)S(1)}, bf16[512,1024]{1,0:T(8,128)(2,1)S(1)}, u32[]{:S(2)}, u32[]{:S(2)}) collective-permute-start(bf16[512,1024]{1,0:T(8,128)(2,1)S(1)} %get-tuple-element.33), channel_id=1, source_target_pairs={{0,4},{1,5},{2,6},{3,7},{4,0},{5,1},{6,2},{7,3},{8,12},{9,13},{10,... | collective-permute-start | bytes 3145736 | tf_op jit(solution)/shard_map/ppermute | solution.py:55
  126.8 21.2 %collective-permute-start.11 = (bf16[2,4,128,256]{3,2,1,0:T(8,128)(2,1)S(1)}, bf16[2,4,128,256]{3,2,1,0:T(8,128)(2,1)S(1)}, u32[]{:S(2)}, u32[]{:S(2)}) collective-permute-start(bf16[2,4,128,256]{3,2,1,0:T(8,128)(2,1)S(1)} %collective-permute-done.10.refs_0_), channel_id=1, source_target_pairs={{0,8},{1,9},{2,10},{3,11},{4,60},{5,61},{6,62},{7,63},{8,16},{9,17... | collective-permute-start | bytes 1572872 | tf_op jit(solution)/shard_map/ppermute | solution.py:55
  128.8 15.4 %collective-permute-start.41 = (bf16[32,2304]{1,0:T(8,128)(2,1)S(1)}, bf16[32,2304]{1,0:T(8,128)(2,1)S(1)}, u32[]{:S(2)}, u32[]{:S(2)}) collective-permute-start(bf16[32,2304]{1,0:T(8,128)(2,1)S(1)} %get-tuple-element.47), channel_id=1, source_target_pairs={{0,56},{1,57},{2,58},{3,59},{4,12},{5,13},{6,14},{7,15},{8,0},{9,1... | collective-permute-start | bytes 442376 | tf_op jit(solution)/shard_map/ppermute | solution.py:55
  128.9 19.0 %collective-permute-start.42 = (bf16[32,2304]{1,0:T(8,128)(2,1)S(1)}, bf16[32,2304]{1,0:T(8,128)(2,1)S(1)}, u32[]{:S(2)}, u32[]{:S(2)}) collective-permute-start(bf16[32,2304]{1,0:T(8,128)(2,1)S(1)} %get-tuple-element.48), channel_id=1, source_target_pairs={{0,48},{1,49},{2,50},{3,51},{4,20},{5,21},{6,22},{7,23},{8,56},{9,... | collective-permute-start | bytes 442376 | tf_op jit(solution)/shard_map/ppermute | solution.py:55
  130.3 13.9 %collective-permute-start.44 = (bf16[16,2304]{1,0:T(8,128)(2,1)S(1)}, bf16[16,2304]{1,0:T(8,128)(2,1)S(1)}, u32[]{:S(2)}, u32[]{:S(2)}) collective-permute-start(bf16[16,2304]{1,0:T(8,128)(2,1)S(1)} %get-tuple-element.50), channel_id=1, source_target_pairs={{0,32},{1,33},{2,34},{3,35},{4,36},{5,37},{6,38},{7,39},{8,40},{9,... | collective-permute-start | bytes 221192 | tf_op jit(solution)/shard_map/ppermute | solution.py:55
  144.2 13.1 %collective-permute-start.1 = (bf16[512,256]{1,0:T(8,128)(2,1)S(1)}, bf16[512,256]{1,0:T(8,128)(2,1)S(1)}, u32[]{:S(2)}, u32[]{:S(2)}) collective-permute-start(bf16[512,256]{1,0:T(8,128)(2,1)S(1)} %get-tuple-element.66), channel_id=1, source_target_pairs={{0,1},{1,2},{2,3},{3,0},{4,5},{5,6},{6,7},{7,4},{8,9},{9,10},{10,1... | collective-permute-start | bytes 786440 | tf_op jit(solution)/shard_map/ppermute | solution.py:55
  144.2 16.3 %collective-permute-start.2 = (bf16[512,256]{1,0:T(8,128)(2,1)S(1)}, bf16[512,256]{1,0:T(8,128)(2,1)S(1)}, u32[]{:S(2)}, u32[]{:S(2)}) collective-permute-start(bf16[512,256]{1,0:T(8,128)(2,1)S(1)} %get-tuple-element.66), channel_id=1, source_target_pairs={{0,2},{1,3},{2,0},{3,1},{4,6},{5,7},{6,4},{7,5},{8,10},{9,11},{10,... | collective-permute-start | bytes 786440 | tf_op jit(solution)/shard_map/ppermute | solution.py:55
  147.9 12.6 %collective-permute-start.3 = (bf16[512,256]{1,0:T(8,128)(2,1)S(1)}, bf16[512,256]{1,0:T(8,128)(2,1)S(1)}, u32[]{:S(2)}, u32[]{:S(2)}) collective-permute-start(bf16[512,256]{1,0:T(8,128)(2,1)S(1)} %get-tuple-element.66), channel_id=1, source_target_pairs={{0,3},{1,0},{2,1},{3,2},{4,7},{5,4},{6,5},{7,6},{8,11},{9,8},{10,9... | collective-permute-start | bytes 786440 | tf_op jit(solution)/shard_map/ppermute | solution.py:55
  147.9 8.8 %collective-permute-start.43 = (bf16[32,2304]{1,0:T(8,128)(2,1)S(1)}, bf16[32,2304]{1,0:T(8,128)(2,1)S(1)}, u32[]{:S(2)}, u32[]{:S(2)}) collective-permute-start(bf16[32,2304]{1,0:T(8,128)(2,1)S(1)} %get-tuple-element.49), channel_id=1, source_target_pairs={{0,40},{1,41},{2,42},{3,43},{4,28},{5,29},{6,30},{7,31},{8,48},{9,... | collective-permute-start | bytes 442376 | tf_op jit(solution)/shard_map/ppermute | solution.py:55
  156.7 9.7 %collective-permute-start.12 = (bf16[4,128,256]{2,1,0:T(8,128)(2,1)S(1)}, bf16[4,128,256]{2,1,0:T(8,128)(2,1)S(1)}, u32[]{:S(2)}, u32[]{:S(2)}) collective-permute-start(bf16[4,128,256]{2,1,0:T(8,128)(2,1)S(1)} %fusion), channel_id=1, source_target_pairs={{0,8},{1,9},{2,10},{3,11},{4,60},{5,61},{6,62},{7,63},{8,16},{9,17... | collective-permute-start | bytes 786440 | tf_op jit(solution)/shard_map/ppermute | solution.py:55
  (28 other events, 166.9 us)

commit v2 on v1

--- a/solution.py
+++ b/solution.py
@@ -139,7 +139,7 @@
     toks = d0.shape[0]
     for h, dr in enumerate((d0, d1)):
         cols = slice(h * toks, (h + 1) * toks)
-        acc[...] = dot_nt(jnp.concatenate([b[...] for b in (b0, b1, b2, b3)], axis=0), dr[...])
+        acc[...] = dot_nt(jnp.concatenate([b[:128, :] for b in (b0, b1, b2, b3)], axis=0), dr[...])
         total = pick_rows(info, slots_ref[:, cols], acc) * coefficient
         out[:, cols] = total
         turned[:, (1 - h) * toks : (2 - h) * toks] = total
@@ -346,9 +346,7 @@
     slot_other = swapped[:, wide].astype(jnp.int32)
     steps = [both_ways_z(chip_ab, k) for k in range(1, 4)]
     steps = [ab] + steps + [both_ways_z(ab, 4)]
-    bz = jnp.concatenate([s[:, width:] for s in steps], axis=0)
     az = jnp.concatenate([s[:, :width] for s in steps], axis=0)
-    ups = [bz] + [along_y(bz, j) for j in range(1, NY)]
     downs = [az] + [along_y(az, j) for j in range(1, NY)]
 
     slot_all = jnp.concatenate([slot_own, slot_other])
@@ -359,7 +357,9 @@
     x0, x1 = layer_input, swap_cores(layer_input)
 
     weight = to_width_plane(dequantize(quant_codes, block_scales))
-    w0 = jnp.stack([weight] + [along_y(weight, j) for j in range(1, NY)])
+    rider = jnp.concatenate([s[:, width:] for s in steps] + [weight], axis=0)
+    ups = [rider] + [along_y(rider, j) for j in range(1, NY)]
+    w0 = jnp.stack([u[128:] for u in ups])
     w1 = both_ways_z(in_order(w0[None], swap_cores(w0)[None]), 1)
     w2 = both_ways_z(w1, 1)
     w3 = both_ways_z(w2, 1)

time: 173 us -> 169 us (0.977)
  waiting for transfers between devices: 70.3 us -> 54.2 us
  local copies, waits for them, and re-layouts: 1.88 us -> 9.51 us
  starting transfers between devices: 70.7 us -> 75.3 us
    ppermute x46 -> x43, waiting for transfers between devices: 70.3 us -> 54.2 us  [routed(): return lax.ppermute(value, ('fsdp', 'tensor'), pairs)]
    unnamed x34 -> x61, local copies, waits for them, and re-layouts: 1.54 us -> 7.83 us
    ppermute x46 -> x43, starting transfers between devices: 70.7 us -> 75.3 us  [routed(): return lax.ppermute(value, ('fsdp', 'tensor'), pairs)]
  transfers between devices with their start and end apart: 46 -> 43, of which waited for: 11 -> 9; matrix products, arithmetic and copies ran while one was open for 2% -> 3% of each run, Pallas kernels for 11% -> 11%
where the time goes in v2:
time: 169 us; the launch traced here: 168 us
  starting transfers between devices  75.3 us (45%)
  waiting for transfers between devices  54.2 us (32%)
  Pallas kernels  22.4 us (13%)
  local copies, waits for them, and re-layouts  9.51 us (6%)
  other arithmetic  5.18 us (3%)
  between operations  1.85 us (1%)
    ppermute x43, starting transfers between devices, routed(): return lax.ppermute(value, ('fsdp', 'tensor'), pairs)  75.3 us
    ppermute x43, waiting for transfers between devices, routed(): return lax.ppermute(value, ('fsdp', 'tensor'), pairs)  54.2 us
    pallas_call x12, Pallas kernels, call(): pl.pallas_call(body, out_shape=outs, in_specs=([SCALARS] if scalars else...  22.4 us
    unnamed x61, local copies, waits for them, and re-layouts  7.83 us
  transfers between devices with their start and end apart: 43, of which 9 were waited for; matrix products, arithmetic and copies ran while one was open for 3% of the time, Pallas kernels for 11%

profile of v2, /device:TPU:1, one launch (start us, length us, event | category | flops | bytes accessed | tf_op | source)
XLA Modules:
  0.0 168.4 jit_solution(9810216738717379789)
XLA Ops:
  1.9 3.3 %collective-permute-start.5 = (bf16[16,2432]{1,0:T(8,128)(2,1)S(1)}, bf16[16,2432]{1,0:T(8,128)(2,1)S(1)}, u32[]{:S(2)}, u32[]{:S(2)}) collective-permute-start(bf16[16,2432]{1,0:T(8,128)(2,1)S(1)} %pad_maximum_fusion.5), channel_id=1, source_target_pairs={{0,4},{1,5},{2,6},{3,7},{4,0},{5,1},{6,2},{7,3},{8,12},{9,13},{10,... | collective-permute-start | bytes 233480 | tf_op jit(solution)/shard_map/ppermute | solution.py:55
  8.1 3.9 %collective-permute-start.6 = (bf16[32,2304]{1,0:T(8,128)(2,1)S(1)}, bf16[32,2304]{1,0:T(8,128)(2,1)S(1)}, u32[]{:S(2)}, u32[]{:S(2)}) collective-permute-start(bf16[32,2304]{1,0:T(8,128)(2,1)S(1)} %pad_maximum_fusion.4), channel_id=1, source_target_pairs={{0,8},{1,9},{2,10},{3,11},{4,60},{5,61},{6,62},{7,63},{8,16},{9,17... | collective-permute-start | bytes 442376 | tf_op jit(solution)/shard_map/ppermute | solution.py:55
  14.2 3.0 %collective-permute-start.8 = (bf16[32,2304]{1,0:T(8,128)(2,1)S(1)}, bf16[32,2304]{1,0:T(8,128)(2,1)S(1)}, u32[]{:S(2)}, u32[]{:S(2)}) collective-permute-start(bf16[32,2304]{1,0:T(8,128)(2,1)S(1)} %pad_maximum_fusion.4), channel_id=1, source_target_pairs={{0,24},{1,25},{2,26},{3,27},{4,44},{5,45},{6,46},{7,47},{8,32},{9,... | collective-permute-start | bytes 442376 | tf_op jit(solution)/shard_map/ppermute | solution.py:55
  18.1 3.7 %collective-permute-start.9 = (bf16[16,2304]{1,0:T(8,128)(2,1)S(1)}, bf16[16,2304]{1,0:T(8,128)(2,1)S(1)}, u32[]{:S(2)}, u32[]{:S(2)}) collective-permute-start(bf16[16,2304]{1,0:T(8,128)(2,1)S(1)} %get-tuple-element.69), channel_id=1, source_target_pairs={{0,32},{1,33},{2,34},{3,35},{4,36},{5,37},{6,38},{7,39},{8,40},{9,... | collective-permute-start | bytes 221192 | tf_op jit(solution)/shard_map/ppermute | solution.py:55
  21.9 4.7 %collective-permute-done.9 = bf16[16,2304]{1,0:T(8,128)(2,1)S(1)} collective-permute-done((bf16[16,2304]{1,0:T(8,128)(2,1)S(1)}, bf16[16,2304]{1,0:T(8,128)(2,1)S(1)}, u32[]{:S(2)}, u32[]{:S(2)}) %collective-permute-start.9) | collective-permute-done | bytes 73760 | tf_op jit(solution)/shard_map/ppermute | solution.py:55
  26.7 2.6 %collective-permute-start.10 = (bf16[256,256]{1,0:T(8,128)(2,1)S(1)}, bf16[256,256]{1,0:T(8,128)(2,1)S(1)}, u32[]{:S(2)}, u32[]{:S(2)}) collective-permute-start(bf16[256,256]{1,0:T(8,128)(2,1)S(1)} %constant_dynamic-update-slice_fusion.b0), channel_id=1, source_target_pairs={{0,64},{1,65},{2,66},{3,67},{4,68},{5,69},{6,70},{7,71},{8,72},{9,... | collective-permute-start | bytes 393224 | tf_op jit(solution)/shard_map/ppermute | solution.py:55
  29.3 3.7 %collective-permute-start.11 = (bf16[256,256]{1,0:T(8,128)(2,1)S(1)}, bf16[256,256]{1,0:T(8,128)(2,1)S(1)}, u32[]{:S(2)}, u32[]{:S(2)}) collective-permute-start(bf16[256,256]{1,0:T(8,128)(2,1)S(1)} %constant_dynamic-update-slice_fusion.b0), channel_id=1, source_target_pairs={{0,128},{1,129},{2,130},{3,131},{4,132},{5,133},{6,134},{7,135},{8... | collective-permute-start | bytes 393224 | tf_op jit(solution)/shard_map/ppermute | solution.py:55
  34.4 2.3 %collective-permute-done.12.b3 = bf16[256,256]{1,0:T(8,128)(2,1)S(1)} collective-permute-done((bf16[256,256]{1,0:T(8,128)(2,1)S(1)}, bf16[256,256]{1,0:T(8,128)(2,1)S(1)}, u32[]{:S(2)}, u32[]{:S(2)}) %collective-permute-start.12) | collective-permute-done | bytes 131104 | tf_op jit(solution)/shard_map/ppermute | solution.py:55
  38.1 7.0 %collective-permute-start.13 = (bf16[4,128,256]{2,1,0:T(8,128)(2,1)S(1)}, bf16[4,128,256]{2,1,0:T(8,128)(2,1)S(1)}, u32[]{:S(2)}, u32[]{:S(2)}) collective-permute-start(bf16[4,128,256]{2,1,0:T(8,128)(2,1)S(1)} %pad_maximum_fusion.3.refs_0_), channel_id=1, source_target_pairs={{0,4},{1,5},{2,6},{3,7},{4,0},{5,1},{6,2},{7,3},{8,12},{9,13},{10,... | collective-permute-start | bytes 786440 | tf_op jit(solution)/shard_map/ppermute | solution.py:55
  45.7 3.2 %collective-permute-start.23 = (bf16[128,2048]{1,0:T(8,128)(2,1)S(1)}, bf16[128,2048]{1,0:T(8,128)(2,1)}, u32[]{:S(2)}, u32[]{:S(2)}) collective-permute-start(bf16[128,2048]{1,0:T(8,128)(2,1)S(1)} %slice_dynamic-update-slice_fusion.3.a0), channel_id=1, source_target_pairs={{0,128},{1,129},{2,130},{3,131},{4,132},{5,133},{6,134},{7,135},{8... | collective-permute-start | bytes 1572872 | tf_op jit(solution)/shard_map/ppermute | solution.py:55
  51.1 3.9 %collective-permute-start.14 = (bf16[2,4,128,256]{3,2,1,0:T(8,128)(2,1)}, bf16[2,4,128,256]{3,2,1,0:T(8,128)(2,1)S(1)}, u32[]{:S(2)}, u32[]{:S(2)}) collective-permute-start(bf16[2,4,128,256]{3,2,1,0:T(8,128)(2,1)} %pad_maximum_fusion.1), channel_id=1, source_target_pairs={{0,8},{1,9},{2,10},{3,11},{4,60},{5,61},{6,62},{7,63},{8,16},{9,17... | collective-permute-start | bytes 1572872 | tf_op jit(solution)/shard_map/ppermute | solution.py:55
  63.3 8.9 %collective-permute-done.23.a2 = bf16[128,2048]{1,0:T(8,128)(2,1)} collective-permute-done((bf16[128,2048]{1,0:T(8,128)(2,1)S(1)}, bf16[128,2048]{1,0:T(8,128)(2,1)}, u32[]{:S(2)}, u32[]{:S(2)}) %collective-permute-start.23) | collective-permute-done | bytes 524320 | tf_op jit(solution)/shard_map/ppermute | solution.py:55
  72.2 3.5 %shard_map.206 = (f32[16,512]{1,0:T(8,128)S(1)}, f32[16,512]{1,0:T(8,128)S(1)}) custom-call(s32[4]{0:T(128)S(1)} %and_select_fusion.1.info, s32[1,512]{1,0:T(1,128)S(1)} %reshape.53.slots_ref, bf16[256,2048]{1,0:T(8,128)(2,1)S(1)} %copy-done, bf16[256,2048]{1,0:T(8,128)(2,1)S(1)} %collective-permute-done.27.x1, ...), custom_call_target="tpu_custom_call" | custom-call | flops 1073741824 | bytes 4261904 | tf_op jit(solution)/shard_map/pallas_call | solution.py:298
  77.8 1.8 %collective-permute-start.20 = (f32[16,512]{1,0:T(8,128)S(1)}, f32[16,512]{1,0:T(8,128)S(1)}, u32[]{:S(2)}, u32[]{:S(2)}) collective-permute-start(f32[16,512]{1,0:T(8,128)S(1)} %add.78), channel_id=1, source_target_pairs={{0,2},{1,3},{2,0},{3,1},{4,6},{5,7},{6,4},{7,5},{8,10},{9,11},{10,... | collective-permute-start | bytes 98312 | tf_op jit(solution)/shard_map/ppermute | solution.py:55
  82.4 1.6 collective-permute-start.34
  84.0 3.7 %collective-permute-start.15 = (bf16[2,4,128,256]{3,2,1,0:T(8,128)(2,1)S(1)}, bf16[2,4,128,256]{3,2,1,0:T(8,128)(2,1)S(1)}, u32[]{:S(2)}, u32[]{:S(2)}) collective-permute-start(bf16[2,4,128,256]{3,2,1,0:T(8,128)(2,1)S(1)} %collective-permute-done.14.refs_1_), channel_id=1, source_target_pairs={{0,8},{1,9},{2,10},{3,11},{4,60},{5,61},{6,62},{7,63},{8,16},{9,17... | collective-permute-start | bytes 1572872 | tf_op jit(solution)/shard_map/ppermute | solution.py:55
  88.6 2.3 %collective-permute-start.35 = (bf16[128,256]{1,0:T(8,128)(2,1)S(1)}, bf16[128,256]{1,0:T(8,128)(2,1)S(1)}, u32[]{:S(2)}, u32[]{:S(2)}) collective-permute-start(bf16[128,256]{1,0:T(8,128)(2,1)S(1)} %get-tuple-element.43), channel_id=1, source_target_pairs={{0,192},{1,193},{2,194},{3,195},{4,196},{5,197},{6,198},{7,199},{8... | collective-permute-start | bytes 196616 | tf_op jit(solution)/shard_map/ppermute | solution.py:55
  91.5 3.1 %shard_map.205 = (bf16[128,2048]{1,0:T(8,128)(2,1)S(1)}, bf16[128,2048]{1,0:T(8,128)(2,1)S(1)}, bf16[128,2048]{1,0:T(8,128)(2,1)S(1)}, bf16[128,2048]{1,0:T(8,128)(2,1)S(1)}) custom-call(s32[4]{0:T(128)S(1)} %and_select_fusion.1.info, s32[1,512]{1,0:T(1,128)S(1)} %reshape.53.slots_ref, bf16[16,512]{1,0:T(8,128)(2,1)S(1)} %add_convert_fusion.1.low_ref, ...), custom_call_target="tpu_custom_call" | custom-call | flops 1073741824 | bytes 4212752 | tf_op jit(solution)/shard_map/pallas_call | solution.py:298
  98.5 4.4 %shard_map.202 = (bf16[512,1024]{1,0:T(8,128)(2,1)S(1)}, bf16[512,1024]{1,0:T(8,128)(2,1)S(1)}) custom-call(s32[4]{0:T(128)S(1)} %and_select_fusion.1.info, s32[1,512]{1,0:T(1,128)S(1)} %reshape.53.slots_ref, bf16[16,512]{1,0:T(8,128)(2,1)S(1)} %add_convert_fusion.1.low_ref, bf16[128,2048]{1,0:T(8,128)(2,1)S(1)} %slice_dynamic-update-slice_fusion.3.a0, ...), custom_call_target="tpu_custom_call" | custom-call | flops 1073741824 | bytes 4212752 | tf_op jit(solution)/shard_map/pallas_call | solution.py:298
  102.9 20.9 %collective-permute-done.37.u3 = bf16[128,256]{1,0:T(8,128)(2,1)S(1)} collective-permute-done((bf16[128,256]{1,0:T(8,128)(2,1)S(1)}, bf16[128,256]{1,0:T(8,128)(2,1)S(1)}, u32[]{:S(2)}, u32[]{:S(2)}) %collective-permute-start.37) | collective-permute-done | bytes 65568 | tf_op jit(solution)/shard_map/ppermute | solution.py:55
  124.3 2.3 %collective-permute-start.16 = (bf16[2,4,128,256]{3,2,1,0:T(8,128)(2,1)S(1)}, bf16[2,4,128,256]{3,2,1,0:T(8,128)(2,1)S(1)}, u32[]{:S(2)}, u32[]{:S(2)}) collective-permute-start(bf16[2,4,128,256]{3,2,1,0:T(8,128)(2,1)S(1)} %collective-permute-done.15.refs_0_), channel_id=1, source_target_pairs={{0,8},{1,9},{2,10},{3,11},{4,60},{5,61},{6,62},{7,63},{8,16},{9,17... | collective-permute-start | bytes 1572872 | tf_op jit(solution)/shard_map/ppermute | solution.py:55
  127.1 3.2 %collective-permute-start.41 = (bf16[16,2304]{1,0:T(8,128)(2,1)S(1)}, bf16[16,2304]{1,0:T(8,128)(2,1)S(1)}, u32[]{:S(2)}, u32[]{:S(2)}) collective-permute-start(bf16[16,2304]{1,0:T(8,128)(2,1)S(1)} %get-tuple-element.50), channel_id=1, source_target_pairs={{0,32},{1,33},{2,34},{3,35},{4,36},{5,37},{6,38},{7,39},{8,40},{9,... | collective-permute-start | bytes 221192 | tf_op jit(solution)/shard_map/ppermute | solution.py:55
  130.3 9.1 %collective-permute-done.41.r4 = bf16[16,2304]{1,0:T(8,128)(2,1)S(1)} collective-permute-done((bf16[16,2304]{1,0:T(8,128)(2,1)S(1)}, bf16[16,2304]{1,0:T(8,128)(2,1)S(1)}, u32[]{:S(2)}, u32[]{:S(2)}) %collective-permute-start.41) | collective-permute-done | bytes 73760 | tf_op jit(solution)/shard_map/ppermute | solution.py:55
  139.4 2.1 %collective-permute-start.2 = (bf16[512,256]{1,0:T(8,128)(2,1)S(1)}, bf16[512,256]{1,0:T(8,128)(2,1)S(1)}, u32[]{:S(2)}, u32[]{:S(2)}) collective-permute-start(bf16[512,256]{1,0:T(8,128)(2,1)S(1)} %get-tuple-element.66), channel_id=1, source_target_pairs={{0,2},{1,3},{2,0},{3,1},{4,6},{5,7},{6,4},{7,5},{8,10},{9,11},{10,... | collective-permute-start | bytes 786440 | tf_op jit(solution)/shard_map/ppermute | solution.py:55
  142.2 3.6 %collective-permute-start.40 = (bf16[32,2304]{1,0:T(8,128)(2,1)S(1)}, bf16[32,2304]{1,0:T(8,128)(2,1)S(1)}, u32[]{:S(2)}, u32[]{:S(2)}) collective-permute-start(bf16[32,2304]{1,0:T(8,128)(2,1)S(1)} %get-tuple-element.49), channel_id=1, source_target_pairs={{0,40},{1,41},{2,42},{3,43},{4,28},{5,29},{6,30},{7,31},{8,48},{9,... | collective-permute-start | bytes 442376 | tf_op jit(solution)/shard_map/ppermute | solution.py:55
  145.8 7.1 %collective-permute-done.40.r3 = bf16[32,2304]{1,0:T(8,128)(2,1)S(1)} collective-permute-done((bf16[32,2304]{1,0:T(8,128)(2,1)S(1)}, bf16[32,2304]{1,0:T(8,128)(2,1)S(1)}, u32[]{:S(2)}, u32[]{:S(2)}) %collective-permute-start.40) | collective-permute-done | bytes 147488 | tf_op jit(solution)/shard_map/ppermute | solution.py:55
  154.0 2.1 %collective-permute-start.42 = (f32[16,2304]{1,0:T(8,128)S(1)}, f32[16,2304]{1,0:T(8,128)S(1)}, u32[]{:S(2)}, u32[]{:S(2)}) collective-permute-start(f32[16,2304]{1,0:T(8,128)S(1)} %get-tuple-element.52), channel_id=1, source_target_pairs={{0,4},{1,5},{2,6},{3,7},{4,0},{5,1},{6,2},{7,3},{8,12},{9,13},{10,... | collective-permute-start | bytes 442376 | tf_op jit(solution)/shard_map/ppermute | solution.py:55
  156.3 1.8 %shard_map.198.b01 = f32[512,384]{1,0:T(8,128)S(1)} custom-call(s32[4]{0:T(128)S(1)} %and_select_fusion.1.info, bf16[4,512,256]{2,1,0:T(8,128)(2,1)S(1)} %pad_maximum_fusion.dv, bf16[4,128,256]{2,1,0:T(8,128)(2,1)S(1)} %pad_maximum_fusion.3.refs_0_, bf16[2,4,128,256]{3,2,1,0:T(8,128)(2,1)S(1)} %collective-permute-done.14.refs_1_), custom_call_target="tpu_custom_call" | custom-call | flops 402653184 | bytes 2621456 | tf_op jit(solution)/shard_map/pallas_call | solution.py:298
  159.8 1.6 shard_map.200.b3
  161.5 1.8 %shard_map.203 = (bf16[256,1024]{1,0:T(8,128)(2,1)S(1)}, bf16[256,1024]{1,0:T(8,128)(2,1)S(1)}) custom-call(s32[4]{0:T(128)S(1)} %and_select_fusion.1.info, bf16[4,512,256]{2,1,0:T(8,128)(2,1)S(1)} %pad_maximum_fusion.dv, bf16[4,128,256]{2,1,0:T(8,128)(2,1)S(1)} %collective-permute-done.17.w4, f32[512,384]{1,0:T(8,128)S(1)} %shard_map.198.b01, ...), custom_call_target="tpu_custom_call" | custom-call | flops 134217728 | bytes 6291472 | tf_op jit(solution)/shard_map/pallas_call | solution.py:298
  163.4 1.7 %collective-permute-start.26 = (bf16[256,1024]{1,0:T(8,128)(2,1)S(1)}, bf16[256,1024]{1,0:T(8,128)(2,1)S(1)}, u32[]{:S(2)}, u32[]{:S(2)}) collective-permute-start(bf16[256,1024]{1,0:T(8,128)(2,1)S(1)} %get-tuple-element.35), channel_id=1, source_target_pairs={{0,4},{1,5},{2,6},{3,7},{4,0},{5,1},{6,2},{7,3},{8,12},{9,13},{10,... | collective-permute-start | bytes 1572872 | tf_op jit(solution)/shard_map/ppermute | solution.py:55
  166.6 1.8 %shard_map.204 = bf16[256,2048]{1,0:T(8,128)(2,1)} custom-call(s32[4]{0:T(128)S(1)} %and_select_fusion.1.info, bf16[256,1024]{1,0:T(8,128)(2,1)S(1)} %get-tuple-element.34.own, bf16[256,1024]{1,0:T(8,128)(2,1)S(1)} %collective-permute-done.26.other), custom_call_target="tpu_custom_call" | custom-call | bytes 2097168 | tf_op jit(solution)/shard_map/pallas_call | solution.py:298
  (163 shorter events, 36.7 us)
Async XLA Ops:
  5.2 66.9 %collective-permute-start.27 = (bf16[256,2048]{1,0:T(8,128)(2,1)}, bf16[256,2048]{1,0:T(8,128)(2,1)S(1)}, u32[]{:S(2)}, u32[]{:S(2)}) collective-permute-start(bf16[256,2048]{1,0:T(8,128)(2,1)} %x0.3), channel_id=1, source_target_pairs={{0,4},{1,5},{2,6},{3,7},{4,0},{5,1},{6,2},{7,3},{8,12},{9,13},{10,... | collective-permute-start | bytes 3145736 | tf_op jit(solution)/shard_map/ppermute | solution.py:55
  6.1 44.3 %collective-permute-start = (bf16[256,256]{1,0:T(8,128)(2,1)S(1)}, bf16[256,256]{1,0:T(8,128)(2,1)S(1)}, u32[]{:S(2)}, u32[]{:S(2)}) collective-permute-start(bf16[256,256]{1,0:T(8,128)(2,1)S(1)} %broadcast_select_fusion.d0), channel_id=1, source_target_pairs={{0,4},{1,5},{2,6},{3,7},{4,0},{5,1},{6,2},{7,3},{8,12},{9,13},{10,... | collective-permute-start | bytes 393224 | tf_op jit(solution)/shard_map/ppermute | solution.py:55
  12.2 14.5 %collective-permute-start.4 = (bf16[128,256]{1,0:T(8,128)(2,1)S(1)}, bf16[128,256]{1,0:T(8,128)(2,1)S(1)}, u32[]{:S(2)}, u32[]{:S(2)}) collective-permute-start(bf16[128,256]{1,0:T(8,128)(2,1)S(1)} %multiply_convert_fusion), channel_id=1, source_target_pairs={{0,0},{1,64},{2,128},{3,192},{4,4},{5,68},{6,132},{7,196},{8,8},{9... | collective-permute-start | bytes 196616 | tf_op jit(solution)/shard_map/ppermute | solution.py:55
  14.2 7.8 %collective-permute-start.8 = (bf16[32,2304]{1,0:T(8,128)(2,1)S(1)}, bf16[32,2304]{1,0:T(8,128)(2,1)S(1)}, u32[]{:S(2)}, u32[]{:S(2)}) collective-permute-start(bf16[32,2304]{1,0:T(8,128)(2,1)S(1)} %pad_maximum_fusion.4), channel_id=1, source_target_pairs={{0,24},{1,25},{2,26},{3,27},{4,44},{5,45},{6,46},{7,47},{8,32},{9,... | collective-permute-start | bytes 442376 | tf_op jit(solution)/shard_map/ppermute | solution.py:55
  18.1 8.5 %collective-permute-start.9 = (bf16[16,2304]{1,0:T(8,128)(2,1)S(1)}, bf16[16,2304]{1,0:T(8,128)(2,1)S(1)}, u32[]{:S(2)}, u32[]{:S(2)}) collective-permute-start(bf16[16,2304]{1,0:T(8,128)(2,1)S(1)} %get-tuple-element.69), channel_id=1, source_target_pairs={{0,32},{1,33},{2,34},{3,35},{4,36},{5,37},{6,38},{7,39},{8,40},{9,... | collective-permute-start | bytes 221192 | tf_op jit(solution)/shard_map/ppermute | solution.py:55
  26.7 10.7 %collective-permute-start.10 = (bf16[256,256]{1,0:T(8,128)(2,1)S(1)}, bf16[256,256]{1,0:T(8,128)(2,1)S(1)}, u32[]{:S(2)}, u32[]{:S(2)}) collective-permute-start(bf16[256,256]{1,0:T(8,128)(2,1)S(1)} %constant_dynamic-update-slice_fusion.b0), channel_id=1, source_target_pairs={{0,64},{1,65},{2,66},{3,67},{4,68},{5,69},{6,70},{7,71},{8,72},{9,... | collective-permute-start | bytes 393224 | tf_op jit(solution)/shard_map/ppermute | solution.py:55
  29.3 7.5 %collective-permute-start.11 = (bf16[256,256]{1,0:T(8,128)(2,1)S(1)}, bf16[256,256]{1,0:T(8,128)(2,1)S(1)}, u32[]{:S(2)}, u32[]{:S(2)}) collective-permute-start(bf16[256,256]{1,0:T(8,128)(2,1)S(1)} %constant_dynamic-update-slice_fusion.b0), channel_id=1, source_target_pairs={{0,128},{1,129},{2,130},{3,131},{4,132},{5,133},{6,134},{7,135},{8... | collective-permute-start | bytes 393224 | tf_op jit(solution)/shard_map/ppermute | solution.py:55
  38.1 10.8 %collective-permute-start.13 = (bf16[4,128,256]{2,1,0:T(8,128)(2,1)S(1)}, bf16[4,128,256]{2,1,0:T(8,128)(2,1)S(1)}, u32[]{:S(2)}, u32[]{:S(2)}) collective-permute-start(bf16[4,128,256]{2,1,0:T(8,128)(2,1)S(1)} %pad_maximum_fusion.3.refs_0_), channel_id=1, source_target_pairs={{0,4},{1,5},{2,6},{3,7},{4,0},{5,1},{6,2},{7,3},{8,12},{9,13},{10,... | collective-permute-start | bytes 786440 | tf_op jit(solution)/shard_map/ppermute | solution.py:55
  45.1 18.0 %collective-permute-start.22 = (bf16[128,2048]{1,0:T(8,128)(2,1)S(1)}, bf16[128,2048]{1,0:T(8,128)(2,1)}, u32[]{:S(2)}, u32[]{:S(2)}) collective-permute-start(bf16[128,2048]{1,0:T(8,128)(2,1)S(1)} %slice_dynamic-update-slice_fusion.3.a0), channel_id=1, source_target_pairs={{0,64},{1,65},{2,66},{3,67},{4,68},{5,69},{6,70},{7,71},{8,72},{9,... | collective-permute-start | bytes 1572872 | tf_op jit(solution)/shard_map/ppermute | solution.py:55
  45.7 26.5 %collective-permute-start.23 = (bf16[128,2048]{1,0:T(8,128)(2,1)S(1)}, bf16[128,2048]{1,0:T(8,128)(2,1)}, u32[]{:S(2)}, u32[]{:S(2)}) collective-permute-start(bf16[128,2048]{1,0:T(8,128)(2,1)S(1)} %slice_dynamic-update-slice_fusion.3.a0), channel_id=1, source_target_pairs={{0,128},{1,129},{2,130},{3,131},{4,132},{5,133},{6,134},{7,135},{8... | collective-permute-start | bytes 1572872 | tf_op jit(solution)/shard_map/ppermute | solution.py:55
  48.9 23.3 %collective-permute-start.24 = (bf16[128,2048]{1,0:T(8,128)(2,1)S(1)}, bf16[128,2048]{1,0:T(8,128)(2,1)}, u32[]{:S(2)}, u32[]{:S(2)}) collective-permute-start(bf16[128,2048]{1,0:T(8,128)(2,1)S(1)} %slice_dynamic-update-slice_fusion.3.a0), channel_id=1, source_target_pairs={{0,192},{1,193},{2,194},{3,195},{4,196},{5,197},{6,198},{7,199},{8... | collective-permute-start | bytes 1572872 | tf_op jit(solution)/shard_map/ppermute | solution.py:55
  51.1 32.9 %collective-permute-start.14 = (bf16[2,4,128,256]{3,2,1,0:T(8,128)(2,1)}, bf16[2,4,128,256]{3,2,1,0:T(8,128)(2,1)S(1)}, u32[]{:S(2)}, u32[]{:S(2)}) collective-permute-start(bf16[2,4,128,256]{3,2,1,0:T(8,128)(2,1)} %pad_maximum_fusion.1), channel_id=1, source_target_pairs={{0,8},{1,9},{2,10},{3,11},{4,60},{5,61},{6,62},{7,63},{8,16},{9,17... | collective-permute-start | bytes 1572872 | tf_op jit(solution)/shard_map/ppermute | solution.py:55
  63.0 13.7 %collective-permute-start.18 = (f32[16,512]{1,0:T(8,128)S(1)}, f32[16,512]{1,0:T(8,128)S(1)}, u32[]{:S(2)}, u32[]{:S(2)}) collective-permute-start(f32[16,512]{1,0:T(8,128)S(1)} %get-tuple-element.31), channel_id=1, source_target_pairs={{0,4},{1,5},{2,6},{3,7},{4,0},{5,1},{6,2},{7,3},{8,12},{9,13},{10,... | collective-permute-start | bytes 98312 | tf_op jit(solution)/shard_map/ppermute | solution.py:55
  79.7 8.0 %collective-permute-start.21 = (f32[16,512]{1,0:T(8,128)S(1)}, f32[16,512]{1,0:T(8,128)S(1)}, u32[]{:S(2)}, u32[]{:S(2)}) collective-permute-start(f32[16,512]{1,0:T(8,128)S(1)} %add.78), channel_id=1, source_target_pairs={{0,3},{1,0},{2,1},{3,2},{4,7},{5,4},{6,5},{7,6},{8,11},{9,8},{10,9... | collective-permute-start | bytes 98312 | tf_op jit(solution)/shard_map/ppermute | solution.py:55
  80.8 6.9 %collective-permute-start.32 = (f32[16,512]{1,0:T(8,128)S(1)}, f32[16,512]{1,0:T(8,128)S(1)}, u32[]{:S(2)}, u32[]{:S(2)}) collective-permute-start(f32[16,512]{1,0:T(8,128)S(1)} %add.82), channel_id=1, source_target_pairs={{0,1},{1,2},{2,3},{3,0},{4,5},{5,6},{6,7},{7,4},{8,9},{9,10},{10,1... | collective-permute-start | bytes 98312 | tf_op jit(solution)/shard_map/ppermute | solution.py:55
  84.0 40.3 %collective-permute-start.15 = (bf16[2,4,128,256]{3,2,1,0:T(8,128)(2,1)S(1)}, bf16[2,4,128,256]{3,2,1,0:T(8,128)(2,1)S(1)}, u32[]{:S(2)}, u32[]{:S(2)}) collective-permute-start(bf16[2,4,128,256]{3,2,1,0:T(8,128)(2,1)S(1)} %collective-permute-done.14.refs_1_), channel_id=1, source_target_pairs={{0,8},{1,9},{2,10},{3,11},{4,60},{5,61},{6,62},{7,63},{8,16},{9,17... | collective-permute-start | bytes 1572872 | tf_op jit(solution)/shard_map/ppermute | solution.py:55
  88.6 8.6 %collective-permute-start.35 = (bf16[128,256]{1,0:T(8,128)(2,1)S(1)}, bf16[128,256]{1,0:T(8,128)(2,1)S(1)}, u32[]{:S(2)}, u32[]{:S(2)}) collective-permute-start(bf16[128,256]{1,0:T(8,128)(2,1)S(1)} %get-tuple-element.43), channel_id=1, source_target_pairs={{0,192},{1,193},{2,194},{3,195},{4,196},{5,197},{6,198},{7,199},{8... | collective-permute-start | bytes 196616 | tf_op jit(solution)/shard_map/ppermute | solution.py:55
  91.0 7.1 %collective-permute-start.36 = (bf16[128,256]{1,0:T(8,128)(2,1)S(1)}, bf16[128,256]{1,0:T(8,128)(2,1)S(1)}, u32[]{:S(2)}, u32[]{:S(2)}) collective-permute-start(bf16[128,256]{1,0:T(8,128)(2,1)S(1)} %get-tuple-element.44), channel_id=1, source_target_pairs={{0,128},{1,129},{2,130},{3,131},{4,132},{5,133},{6,134},{7,135},{8... | collective-permute-start | bytes 196616 | tf_op jit(solution)/shard_map/ppermute | solution.py:55
  94.7 31.9 %collective-permute-start.28 = (bf16[128,2048]{1,0:T(8,128)(2,1)S(1)}, bf16[128,2048]{1,0:T(8,128)(2,1)S(1)}, u32[]{:S(2)}, u32[]{:S(2)}) collective-permute-start(bf16[128,2048]{1,0:T(8,128)(2,1)S(1)} %get-tuple-element.37), channel_id=1, source_target_pairs={{0,192},{1,193},{2,194},{3,195},{4,196},{5,197},{6,198},{7,199},{8... | collective-permute-start | bytes 1572872 | tf_op jit(solution)/shard_map/ppermute | solution.py:55
  95.8 30.8 %collective-permute-start.29 = (bf16[128,2048]{1,0:T(8,128)(2,1)S(1)}, bf16[128,2048]{1,0:T(8,128)(2,1)S(1)}, u32[]{:S(2)}, u32[]{:S(2)}) collective-permute-start(bf16[128,2048]{1,0:T(8,128)(2,1)S(1)} %get-tuple-element.38), channel_id=1, source_target_pairs={{0,128},{1,129},{2,130},{3,131},{4,132},{5,133},{6,134},{7,135},{8... | collective-permute-start | bytes 1572872 | tf_op jit(solution)/shard_map/ppermute | solution.py:55
  97.3 29.3 %collective-permute-start.30 = (bf16[128,2048]{1,0:T(8,128)(2,1)S(1)}, bf16[128,2048]{1,0:T(8,128)(2,1)S(1)}, u32[]{:S(2)}, u32[]{:S(2)}) collective-permute-start(bf16[128,2048]{1,0:T(8,128)(2,1)S(1)} %get-tuple-element.39), channel_id=1, source_target_pairs={{0,64},{1,65},{2,66},{3,67},{4,68},{5,69},{6,70},{7,71},{8,72},{9,... | collective-permute-start | bytes 1572872 | tf_op jit(solution)/shard_map/ppermute | solution.py:55
  98.0 25.8 %collective-permute-start.37 = (bf16[128,256]{1,0:T(8,128)(2,1)S(1)}, bf16[128,256]{1,0:T(8,128)(2,1)S(1)}, u32[]{:S(2)}, u32[]{:S(2)}) collective-permute-start(bf16[128,256]{1,0:T(8,128)(2,1)S(1)} %get-tuple-element.45), channel_id=1, source_target_pairs={{0,64},{1,65},{2,66},{3,67},{4,68},{5,69},{6,70},{7,71},{8,72},{9,... | collective-permute-start | bytes 196616 | tf_op jit(solution)/shard_map/ppermute | solution.py:55
  123.8 37.6 %collective-permute-start.25 = (bf16[512,1024]{1,0:T(8,128)(2,1)S(1)}, bf16[512,1024]{1,0:T(8,128)(2,1)S(1)}, u32[]{:S(2)}, u32[]{:S(2)}) collective-permute-start(bf16[512,1024]{1,0:T(8,128)(2,1)S(1)} %get-tuple-element.33), channel_id=1, source_target_pairs={{0,4},{1,5},{2,6},{3,7},{4,0},{5,1},{6,2},{7,3},{8,12},{9,13},{10,... | collective-permute-start | bytes 3145736 | tf_op jit(solution)/shard_map/ppermute | solution.py:55
  124.3 17.9 %collective-permute-start.16 = (bf16[2,4,128,256]{3,2,1,0:T(8,128)(2,1)S(1)}, bf16[2,4,128,256]{3,2,1,0:T(8,128)(2,1)S(1)}, u32[]{:S(2)}, u32[]{:S(2)}) collective-permute-start(bf16[2,4,128,256]{3,2,1,0:T(8,128)(2,1)S(1)} %collective-permute-done.15.refs_0_), channel_id=1, source_target_pairs={{0,8},{1,9},{2,10},{3,11},{4,60},{5,61},{6,62},{7,63},{8,16},{9,17... | collective-permute-start | bytes 1572872 | tf_op jit(solution)/shard_map/ppermute | solution.py:55
  126.9 12.5 %collective-permute-start.38 = (bf16[32,2304]{1,0:T(8,128)(2,1)S(1)}, bf16[32,2304]{1,0:T(8,128)(2,1)S(1)}, u32[]{:S(2)}, u32[]{:S(2)}) collective-permute-start(bf16[32,2304]{1,0:T(8,128)(2,1)S(1)} %get-tuple-element.47), channel_id=1, source_target_pairs={{0,56},{1,57},{2,58},{3,59},{4,12},{5,13},{6,14},{7,15},{8,0},{9,1... | collective-permute-start | bytes 442376 | tf_op jit(solution)/shard_map/ppermute | solution.py:55
  127.0 14.6 %collective-permute-start.39 = (bf16[32,2304]{1,0:T(8,128)(2,1)S(1)}, bf16[32,2304]{1,0:T(8,128)(2,1)S(1)}, u32[]{:S(2)}, u32[]{:S(2)}) collective-permute-start(bf16[32,2304]{1,0:T(8,128)(2,1)S(1)} %get-tuple-element.48), channel_id=1, source_target_pairs={{0,48},{1,49},{2,50},{3,51},{4,20},{5,21},{6,22},{7,23},{8,56},{9,... | collective-permute-start | bytes 442376 | tf_op jit(solution)/shard_map/ppermute | solution.py:55
  127.1 12.3 %collective-permute-start.41 = (bf16[16,2304]{1,0:T(8,128)(2,1)S(1)}, bf16[16,2304]{1,0:T(8,128)(2,1)S(1)}, u32[]{:S(2)}, u32[]{:S(2)}) collective-permute-start(bf16[16,2304]{1,0:T(8,128)(2,1)S(1)} %get-tuple-element.50), channel_id=1, source_target_pairs={{0,32},{1,33},{2,34},{3,35},{4,36},{5,37},{6,38},{7,39},{8,40},{9,... | collective-permute-start | bytes 221192 | tf_op jit(solution)/shard_map/ppermute | solution.py:55
  139.4 14.6 %collective-permute-start.1 = (bf16[512,256]{1,0:T(8,128)(2,1)S(1)}, bf16[512,256]{1,0:T(8,128)(2,1)S(1)}, u32[]{:S(2)}, u32[]{:S(2)}) collective-permute-start(bf16[512,256]{1,0:T(8,128)(2,1)S(1)} %get-tuple-element.66), channel_id=1, source_target_pairs={{0,1},{1,2},{2,3},{3,0},{4,5},{5,6},{6,7},{7,4},{8,9},{9,10},{10,1... | collective-permute-start | bytes 786440 | tf_op jit(solution)/shard_map/ppermute | solution.py:55
  139.4 16.7 %collective-permute-start.2 = (bf16[512,256]{1,0:T(8,128)(2,1)S(1)}, bf16[512,256]{1,0:T(8,128)(2,1)S(1)}, u32[]{:S(2)}, u32[]{:S(2)}) collective-permute-start(bf16[512,256]{1,0:T(8,128)(2,1)S(1)} %get-tuple-element.66), channel_id=1, source_target_pairs={{0,2},{1,3},{2,0},{3,1},{4,6},{5,7},{6,4},{7,5},{8,10},{9,11},{10,... | collective-permute-start | bytes 786440 | tf_op jit(solution)/shard_map/ppermute | solution.py:55
  141.5 14.6 %collective-permute-start.3 = (bf16[512,256]{1,0:T(8,128)(2,1)S(1)}, bf16[512,256]{1,0:T(8,128)(2,1)S(1)}, u32[]{:S(2)}, u32[]{:S(2)}) collective-permute-start(bf16[512,256]{1,0:T(8,128)(2,1)S(1)} %get-tuple-element.66), channel_id=1, source_target_pairs={{0,3},{1,0},{2,1},{3,2},{4,7},{5,4},{6,5},{7,6},{8,11},{9,8},{10,9... | collective-permute-start | bytes 786440 | tf_op jit(solution)/shard_map/ppermute | solution.py:55
  142.2 10.7 %collective-permute-start.40 = (bf16[32,2304]{1,0:T(8,128)(2,1)S(1)}, bf16[32,2304]{1,0:T(8,128)(2,1)S(1)}, u32[]{:S(2)}, u32[]{:S(2)}) collective-permute-start(bf16[32,2304]{1,0:T(8,128)(2,1)S(1)} %get-tuple-element.49), channel_id=1, source_target_pairs={{0,40},{1,41},{2,42},{3,43},{4,28},{5,29},{6,30},{7,31},{8,48},{9,... | collective-permute-start | bytes 442376 | tf_op jit(solution)/shard_map/ppermute | solution.py:55
  152.9 8.5 %collective-permute-start.17 = (bf16[4,128,256]{2,1,0:T(8,128)(2,1)S(1)}, bf16[4,128,256]{2,1,0:T(8,128)(2,1)S(1)}, u32[]{:S(2)}, u32[]{:S(2)}) collective-permute-start(bf16[4,128,256]{2,1,0:T(8,128)(2,1)S(1)} %fusion), channel_id=1, source_target_pairs={{0,8},{1,9},{2,10},{3,11},{4,60},{5,61},{6,62},{7,63},{8,16},{9,17... | collective-permute-start | bytes 786440 | tf_op jit(solution)/shard_map/ppermute | solution.py:55
  (38 other events, 144.0 us)
